TPU v7x, 128 devices: a whole 4x4x4 slice. The times are simulated.
128 devices in a mesh: layer: 32 (over x, y, core), rows: 4 (over z).
Axes of the slice: x: 4, y: 4, z: 4, core: 2. Of those that a mesh axis runs over, the one named last changes fastest.
Arguments:
- weights: bfloat16 [256, 32, 288], P('layer'), may hold values from -0.375 to 0.375
- image: float32 [3, 32, 64, 128], P(None, None, 'rows'), may hold values from -6 to 6
- guess: float32 [64, 3, 32, 64, 128], P('layer', None, None, 'rows'), may hold values from -6 to 6
Outputs:
- corrected: float32 [64, 3, 32, 64, 128], P('layer', None, None, 'rows')
All inputs are finite; a program needn't handle non-finite values.
Results may differ from a plain program's by a relative error of at most 0.009.
Values may be sent and summed in bfloat16 or wider, within the bound.
No kernel may reach another device: no remote copies, remote signals or barrier semaphores. Data moves between devices by JAX's collectives and lax.ppermute only.
A program may use at most 64 MiB of HBM per device.

v0:
```python
import jax
import jax.numpy as jnp
from jax import lax
from jax.sharding import PartitionSpec as P

M = 4


step_size = 0.125


def extended_2(block, sides, width):
    for axis, dim in sides:
        count = lax.axis_size(axis)
        forward = [(i, i + 1) for i in range(count - 1)]
        backward = [(target, source) for source, target in forward]
        low = lax.ppermute(
            lax.slice_in_dim(block, block.shape[dim] - width, None, axis=dim), axis, forward
        )
        high = lax.ppermute(lax.slice_in_dim(block, 0, width, axis=dim), axis, backward)
        block = jnp.concatenate([low, block, high], axis=dim)
    return block


def passed_along(value, axis, by):
    size = lax.axis_size(axis)
    pairs = [(i, i + by) for i in range(size) if 0 <= i + by < size]
    return lax.ppermute(value, axis, pairs)


def convolve(extended, matrices):
    padded = jnp.pad(extended, ((0, 0), (0, 0), (0, 0), (0, 0), (1, 1)))
    height = extended.shape[3] - 2
    breadth = extended.shape[4]
    patches = jnp.concatenate(
        [
            padded[:, :, :, row_off : row_off + height, col_off : col_off + breadth]
            for row_off in range(3)
            for col_off in range(3)
        ],
        axis=2,
    )
    return jnp.einsum("iok,inkrw->inorw", matrices, patches, preferred_element_type=jnp.float32)


def edge_rows(field, depth):
    return jnp.concatenate([field[..., :depth, :], field[..., -depth:, :]], axis=-2)


def attach(field, framed, depth):
    return jnp.concatenate([framed[..., :depth, :], field, framed[..., -depth:, :]], axis=-2)


def relax_halo(field):
    lowered = field.astype(jnp.bfloat16)
    framed = extended_2(edge_rows(lowered, 1), (("rows", 3),), 1)
    return attach(lowered, framed, 1)


def relax(anchors, grouped, stride):
    opening = convolve(relax_halo(anchors), grouped[:, 0])
    current = anchors + stride * jnp.tanh(opening)
    for layer in range(1, M):
        current = current + stride * jnp.tanh(convolve(relax_halo(current), grouped[:, layer]))
    return current - (anchors + M * stride * jnp.tanh(opening))


def advance(incoming, defects, coarse_w, stride):
    levels = coarse_w.shape[0]
    results = []
    current = incoming
    for point in range(levels):
        lowered = current.astype(jnp.bfloat16)[None]
        framed = extended_2(edge_rows(lowered, 1), (("rows", 3),), 1)
        rimmed = attach(lowered, framed, 1)
        current = (
            current
            + M * stride * jnp.tanh(convolve(rimmed, coarse_w[point][None])[0])
            + defects[point]
        )
        results.append(current)
    return jnp.stack(results)


def per_device(weights, image, guess):
    layers_dev = weights.shape[0]
    levels = layers_dev // M
    sections = lax.axis_size("layer")
    grouped = weights.reshape(levels, M, weights.shape[1], weights.shape[2])
    coarse_w = grouped[:, 0]
    section = lax.axis_index("layer")
    previous = passed_along(guess[levels - 1], "layer", 1)
    opening_state = jnp.where(section == 0, image, previous)
    anchors = jnp.concatenate([opening_state[None], guess[:-1]], axis=0)
    defects = relax(anchors, grouped, step_size)

    def sweep(index, carry):
        incoming, results = carry
        fresh = advance(incoming, defects, coarse_w, step_size)
        sent = passed_along(fresh[levels - 1], "layer", 1)
        return (jnp.where(section == 0, image, sent), fresh)

    _, corrected = lax.fori_loop(0, sections, sweep, (opening_state, jnp.zeros_like(guess)))
    return corrected


def solution(mesh):
    return jax.shard_map(
        per_device,
        mesh=mesh,
        in_specs=(
            P("layer", None, None),
            P(None, None, "rows", None),
            P("layer", None, None, "rows", None),
        ),
        out_specs=P("layer", None, None, "rows", None),
        check_vma=False,
    )
```

profile of v0, /device:TPU:100, one launch (start us, length us, event | category | flops | bytes accessed | tf_op | source)
XLA Modules:
  0.0 1272.3 jit_solution(6459652838726019104)
XLA Ops:
  4.1 13.3 %collective-permute-done.5 = f32[3,32,16,128]{3,1,2,0:T(8,128)} collective-permute-done((f32[3,32,16,128]{3,1,2,0:T(8,128)S(1)}, f32[3,32,16,128]{3,1,2,0:T(8,128)}, u32[]{:S(2)}, u32[]{:S(2)}) %collective-permute-start.5) | collective-permute-done | bytes 786464 | tf_op jit(solution)/shard_map/ppermute | solution.py:28
  21.1 4.5 collective-permute-start.7
  33.5 4.9 collective-permute-start.9
  46.0 5.1 collective-permute-start.11
  59.7 4.9 collective-permute-start.13
  71.7 1197.1 %while.14 = (s32[]{:T(128)}, f32[3,32,16,128]{3,1,2,0:T(8,128)S(1)}, f32[2,3,32,16,128]{4,2,3,1,0:T(8,128)}, pred[]{:T(512)}, bf16[2,32,288]{2,1,0:T(8,128)(2,1)...) while((s32[]{:T(128)}, f32[3,32,16,128]{3,1,2,0:T(8,128)S(1)}, ...), condition=%wide.region_1.2_spmd, body=%wide.region_0.1_spmd.sunk | while | flops 237585408 | bytes 43415352 | solution.py:103
  71.8 4.2 collective-permute-start
  77.5 4.2 collective-permute-done.1
  89.7 4.2 collective-permute-done.3
  99.7 12.2 collective-permute-done.4
  118.8 4.2 collective-permute-done.1
  129.0 4.2 collective-permute-done.3
  138.9 12.2 collective-permute-done.4
  156.0 4.2 collective-permute-done.1
  166.2 4.2 collective-permute-done.3
  176.2 12.2 collective-permute-done.4
  213.4 12.2 collective-permute-done.4
  250.6 12.2 collective-permute-done.4
  287.8 12.2 collective-permute-done.4
  325.0 12.2 collective-permute-done.4
  362.2 12.2 collective-permute-done.4
  399.4 12.2 collective-permute-done.4
  436.6 12.2 collective-permute-done.4
  473.9 12.2 collective-permute-done.4
  511.1 12.2 collective-permute-done.4
  538.3 4.2 collective-permute-done.3
  548.3 12.2 collective-permute-done.4
  585.5 12.2 collective-permute-done.4
  622.7 12.2 collective-permute-done.4
  659.9 12.2 collective-permute-done.4
  697.1 12.2 collective-permute-done.4
  734.3 12.2 collective-permute-done.4
  771.6 12.2 collective-permute-done.4
  808.8 12.2 collective-permute-done.4
  846.0 12.2 collective-permute-done.4
  863.0 4.2 collective-permute-done.1
  883.2 12.2 collective-permute-done.4
  920.4 12.2 collective-permute-done.4
  957.6 12.2 collective-permute-done.4
  994.8 12.2 collective-permute-done.4
  1032.0 12.2 collective-permute-done.4
  1069.3 12.2 collective-permute-done.4
  1106.5 12.2 collective-permute-done.4
  1143.7 12.2 collective-permute-done.4
  1180.9 12.2 collective-permute-done.4
  1218.1 12.2 collective-permute-done.4
  1245.3 4.2 collective-permute-done.3
  1255.3 12.2 collective-permute-done.4
  (1317 shorter events, 799.1 us)
Async XLA Ops:
  1.9 15.5 %collective-permute-start.5 = (f32[3,32,16,128]{3,1,2,0:T(8,128)S(1)}, f32[3,32,16,128]{3,1,2,0:T(8,128)}, u32[]{:S(2)}, u32[]{:S(2)}) collective-permute-start(f32[3,32,16,128]{3,1,2,0:T(8,128)S(1)} %bitcast.180), channel_id=1, source_target_pairs={{0,4},{4,8},{8,12},{12,16},{16,20},{20,24},{24,28},{28,32},{32,36}... | collective-permute-start | bytes 2359304 | tf_op jit(solution)/shard_map/ppermute | solution.py:28
  19.8 6.0 collective-permute-start.6
  21.1 6.3 collective-permute-start.7
  32.2 6.3 collective-permute-start.8
  33.5 6.6 collective-permute-start.9
  44.7 6.4 collective-permute-start.10
  46.0 6.6 collective-permute-start.11
  58.4 6.3 collective-permute-start.12
  59.7 6.6 collective-permute-start.13
  71.8 5.8 collective-permute-start
  76.0 5.7 collective-permute-start.1
  88.2 5.7 collective-permute-start.3
  96.4 15.5 %collective-permute-start.4 = (f32[3,32,16,128]{3,1,2,0:T(8,128)S(1)}, f32[3,32,16,128]{3,1,2,0:T(8,128)}, u32[]{:S(2)}, u32[]{:S(2)}) collective-permute-start(f32[3,32,16,128]{3,1,2,0:T(8,128)S(1)} %fusion.95), channel_id=1, source_target_pairs={{0,4},{4,8},{8,12},{12,16},{16,20},{20,24},{24,28},{28,32},{32,36}... | collective-permute-start | bytes 2359304 | tf_op jit(solution)/shard_map/while/body/eval_jaxpr/ppermute | solution.py:28
  135.6 15.5 %collective-permute-start.4 = (f32[3,32,16,128]{3,1,2,0:T(8,128)S(1)}, f32[3,32,16,128]{3,1,2,0:T(8,128)}, u32[]{:S(2)}, u32[]{:S(2)}) collective-permute-start(f32[3,32,16,128]{3,1,2,0:T(8,128)S(1)} %fusion.95), channel_id=1, source_target_pairs={{0,4},{4,8},{8,12},{12,16},{16,20},{20,24},{24,28},{28,32},{32,36}... | collective-permute-start | bytes 2359304 | tf_op jit(solution)/shard_map/while/body/eval_jaxpr/ppermute | solution.py:28
  154.5 5.7 collective-permute-start.1
  164.7 5.7 collective-permute-start.3
  172.9 15.5 %collective-permute-start.4 = (f32[3,32,16,128]{3,1,2,0:T(8,128)S(1)}, f32[3,32,16,128]{3,1,2,0:T(8,128)}, u32[]{:S(2)}, u32[]{:S(2)}) collective-permute-start(f32[3,32,16,128]{3,1,2,0:T(8,128)S(1)} %fusion.95), channel_id=1, source_target_pairs={{0,4},{4,8},{8,12},{12,16},{16,20},{20,24},{24,28},{28,32},{32,36}... | collective-permute-start | bytes 2359304 | tf_op jit(solution)/shard_map/while/body/eval_jaxpr/ppermute | solution.py:28
  210.1 15.5 %collective-permute-start.4 = (f32[3,32,16,128]{3,1,2,0:T(8,128)S(1)}, f32[3,32,16,128]{3,1,2,0:T(8,128)}, u32[]{:S(2)}, u32[]{:S(2)}) collective-permute-start(f32[3,32,16,128]{3,1,2,0:T(8,128)S(1)} %fusion.95), channel_id=1, source_target_pairs={{0,4},{4,8},{8,12},{12,16},{16,20},{20,24},{24,28},{28,32},{32,36}... | collective-permute-start | bytes 2359304 | tf_op jit(solution)/shard_map/while/body/eval_jaxpr/ppermute | solution.py:28
  228.9 5.7 collective-permute-start.1
  247.3 15.5 %collective-permute-start.4 = (f32[3,32,16,128]{3,1,2,0:T(8,128)S(1)}, f32[3,32,16,128]{3,1,2,0:T(8,128)}, u32[]{:S(2)}, u32[]{:S(2)}) collective-permute-start(f32[3,32,16,128]{3,1,2,0:T(8,128)S(1)} %fusion.95), channel_id=1, source_target_pairs={{0,4},{4,8},{8,12},{12,16},{16,20},{20,24},{24,28},{28,32},{32,36}... | collective-permute-start | bytes 2359304 | tf_op jit(solution)/shard_map/while/body/eval_jaxpr/ppermute | solution.py:28
  284.5 15.5 %collective-permute-start.4 = (f32[3,32,16,128]{3,1,2,0:T(8,128)S(1)}, f32[3,32,16,128]{3,1,2,0:T(8,128)}, u32[]{:S(2)}, u32[]{:S(2)}) collective-permute-start(f32[3,32,16,128]{3,1,2,0:T(8,128)S(1)} %fusion.95), channel_id=1, source_target_pairs={{0,4},{4,8},{8,12},{12,16},{16,20},{20,24},{24,28},{28,32},{32,36}... | collective-permute-start | bytes 2359304 | tf_op jit(solution)/shard_map/while/body/eval_jaxpr/ppermute | solution.py:28
  321.7 15.5 %collective-permute-start.4 = (f32[3,32,16,128]{3,1,2,0:T(8,128)S(1)}, f32[3,32,16,128]{3,1,2,0:T(8,128)}, u32[]{:S(2)}, u32[]{:S(2)}) collective-permute-start(f32[3,32,16,128]{3,1,2,0:T(8,128)S(1)} %fusion.95), channel_id=1, source_target_pairs={{0,4},{4,8},{8,12},{12,16},{16,20},{20,24},{24,28},{28,32},{32,36}... | collective-permute-start | bytes 2359304 | tf_op jit(solution)/shard_map/while/body/eval_jaxpr/ppermute | solution.py:28
  350.7 5.7 collective-permute-start.3
  358.9 15.5 %collective-permute-start.4 = (f32[3,32,16,128]{3,1,2,0:T(8,128)S(1)}, f32[3,32,16,128]{3,1,2,0:T(8,128)}, u32[]{:S(2)}, u32[]{:S(2)}) collective-permute-start(f32[3,32,16,128]{3,1,2,0:T(8,128)S(1)} %fusion.95), channel_id=1, source_target_pairs={{0,4},{4,8},{8,12},{12,16},{16,20},{20,24},{24,28},{28,32},{32,36}... | collective-permute-start | bytes 2359304 | tf_op jit(solution)/shard_map/while/body/eval_jaxpr/ppermute | solution.py:28
  396.1 15.5 %collective-permute-start.4 = (f32[3,32,16,128]{3,1,2,0:T(8,128)S(1)}, f32[3,32,16,128]{3,1,2,0:T(8,128)}, u32[]{:S(2)}, u32[]{:S(2)}) collective-permute-start(f32[3,32,16,128]{3,1,2,0:T(8,128)S(1)} %fusion.95), channel_id=1, source_target_pairs={{0,4},{4,8},{8,12},{12,16},{16,20},{20,24},{24,28},{28,32},{32,36}... | collective-permute-start | bytes 2359304 | tf_op jit(solution)/shard_map/while/body/eval_jaxpr/ppermute | solution.py:28
  433.3 15.5 %collective-permute-start.4 = (f32[3,32,16,128]{3,1,2,0:T(8,128)S(1)}, f32[3,32,16,128]{3,1,2,0:T(8,128)}, u32[]{:S(2)}, u32[]{:S(2)}) collective-permute-start(f32[3,32,16,128]{3,1,2,0:T(8,128)S(1)} %fusion.95), channel_id=1, source_target_pairs={{0,4},{4,8},{8,12},{12,16},{16,20},{20,24},{24,28},{28,32},{32,36}... | collective-permute-start | bytes 2359304 | tf_op jit(solution)/shard_map/while/body/eval_jaxpr/ppermute | solution.py:28
  470.6 15.5 %collective-permute-start.4 = (f32[3,32,16,128]{3,1,2,0:T(8,128)S(1)}, f32[3,32,16,128]{3,1,2,0:T(8,128)}, u32[]{:S(2)}, u32[]{:S(2)}) collective-permute-start(f32[3,32,16,128]{3,1,2,0:T(8,128)S(1)} %fusion.95), channel_id=1, source_target_pairs={{0,4},{4,8},{8,12},{12,16},{16,20},{20,24},{24,28},{28,32},{32,36}... | collective-permute-start | bytes 2359304 | tf_op jit(solution)/shard_map/while/body/eval_jaxpr/ppermute | solution.py:28
  507.8 15.5 %collective-permute-start.4 = (f32[3,32,16,128]{3,1,2,0:T(8,128)S(1)}, f32[3,32,16,128]{3,1,2,0:T(8,128)}, u32[]{:S(2)}, u32[]{:S(2)}) collective-permute-start(f32[3,32,16,128]{3,1,2,0:T(8,128)S(1)} %fusion.95), channel_id=1, source_target_pairs={{0,4},{4,8},{8,12},{12,16},{16,20},{20,24},{24,28},{28,32},{32,36}... | collective-permute-start | bytes 2359304 | tf_op jit(solution)/shard_map/while/body/eval_jaxpr/ppermute | solution.py:28
  545.0 15.5 %collective-permute-start.4 = (f32[3,32,16,128]{3,1,2,0:T(8,128)S(1)}, f32[3,32,16,128]{3,1,2,0:T(8,128)}, u32[]{:S(2)}, u32[]{:S(2)}) collective-permute-start(f32[3,32,16,128]{3,1,2,0:T(8,128)S(1)} %fusion.95), channel_id=1, source_target_pairs={{0,4},{4,8},{8,12},{12,16},{16,20},{20,24},{24,28},{28,32},{32,36}... | collective-permute-start | bytes 2359304 | tf_op jit(solution)/shard_map/while/body/eval_jaxpr/ppermute | solution.py:28
  582.2 15.5 %collective-permute-start.4 = (f32[3,32,16,128]{3,1,2,0:T(8,128)S(1)}, f32[3,32,16,128]{3,1,2,0:T(8,128)}, u32[]{:S(2)}, u32[]{:S(2)}) collective-permute-start(f32[3,32,16,128]{3,1,2,0:T(8,128)S(1)} %fusion.95), channel_id=1, source_target_pairs={{0,4},{4,8},{8,12},{12,16},{16,20},{20,24},{24,28},{28,32},{32,36}... | collective-permute-start | bytes 2359304 | tf_op jit(solution)/shard_map/while/body/eval_jaxpr/ppermute | solution.py:28
  619.4 15.5 %collective-permute-start.4 = (f32[3,32,16,128]{3,1,2,0:T(8,128)S(1)}, f32[3,32,16,128]{3,1,2,0:T(8,128)}, u32[]{:S(2)}, u32[]{:S(2)}) collective-permute-start(f32[3,32,16,128]{3,1,2,0:T(8,128)S(1)} %fusion.95), channel_id=1, source_target_pairs={{0,4},{4,8},{8,12},{12,16},{16,20},{20,24},{24,28},{28,32},{32,36}... | collective-permute-start | bytes 2359304 | tf_op jit(solution)/shard_map/while/body/eval_jaxpr/ppermute | solution.py:28
  656.6 15.5 %collective-permute-start.4 = (f32[3,32,16,128]{3,1,2,0:T(8,128)S(1)}, f32[3,32,16,128]{3,1,2,0:T(8,128)}, u32[]{:S(2)}, u32[]{:S(2)}) collective-permute-start(f32[3,32,16,128]{3,1,2,0:T(8,128)S(1)} %fusion.95), channel_id=1, source_target_pairs={{0,4},{4,8},{8,12},{12,16},{16,20},{20,24},{24,28},{28,32},{32,36}... | collective-permute-start | bytes 2359304 | tf_op jit(solution)/shard_map/while/body/eval_jaxpr/ppermute | solution.py:28
  693.8 15.5 %collective-permute-start.4 = (f32[3,32,16,128]{3,1,2,0:T(8,128)S(1)}, f32[3,32,16,128]{3,1,2,0:T(8,128)}, u32[]{:S(2)}, u32[]{:S(2)}) collective-permute-start(f32[3,32,16,128]{3,1,2,0:T(8,128)S(1)} %fusion.95), channel_id=1, source_target_pairs={{0,4},{4,8},{8,12},{12,16},{16,20},{20,24},{24,28},{28,32},{32,36}... | collective-permute-start | bytes 2359304 | tf_op jit(solution)/shard_map/while/body/eval_jaxpr/ppermute | solution.py:28
  731.0 15.5 %collective-permute-start.4 = (f32[3,32,16,128]{3,1,2,0:T(8,128)S(1)}, f32[3,32,16,128]{3,1,2,0:T(8,128)}, u32[]{:S(2)}, u32[]{:S(2)}) collective-permute-start(f32[3,32,16,128]{3,1,2,0:T(8,128)S(1)} %fusion.95), channel_id=1, source_target_pairs={{0,4},{4,8},{8,12},{12,16},{16,20},{20,24},{24,28},{28,32},{32,36}... | collective-permute-start | bytes 2359304 | tf_op jit(solution)/shard_map/while/body/eval_jaxpr/ppermute | solution.py:28
  768.3 15.5 %collective-permute-start.4 = (f32[3,32,16,128]{3,1,2,0:T(8,128)S(1)}, f32[3,32,16,128]{3,1,2,0:T(8,128)}, u32[]{:S(2)}, u32[]{:S(2)}) collective-permute-start(f32[3,32,16,128]{3,1,2,0:T(8,128)S(1)} %fusion.95), channel_id=1, source_target_pairs={{0,4},{4,8},{8,12},{12,16},{16,20},{20,24},{24,28},{28,32},{32,36}... | collective-permute-start | bytes 2359304 | tf_op jit(solution)/shard_map/while/body/eval_jaxpr/ppermute | solution.py:28
  805.5 15.5 %collective-permute-start.4 = (f32[3,32,16,128]{3,1,2,0:T(8,128)S(1)}, f32[3,32,16,128]{3,1,2,0:T(8,128)}, u32[]{:S(2)}, u32[]{:S(2)}) collective-permute-start(f32[3,32,16,128]{3,1,2,0:T(8,128)S(1)} %fusion.95), channel_id=1, source_target_pairs={{0,4},{4,8},{8,12},{12,16},{16,20},{20,24},{24,28},{28,32},{32,36}... | collective-permute-start | bytes 2359304 | tf_op jit(solution)/shard_map/while/body/eval_jaxpr/ppermute | solution.py:28
  842.7 15.5 %collective-permute-start.4 = (f32[3,32,16,128]{3,1,2,0:T(8,128)S(1)}, f32[3,32,16,128]{3,1,2,0:T(8,128)}, u32[]{:S(2)}, u32[]{:S(2)}) collective-permute-start(f32[3,32,16,128]{3,1,2,0:T(8,128)S(1)} %fusion.95), channel_id=1, source_target_pairs={{0,4},{4,8},{8,12},{12,16},{16,20},{20,24},{24,28},{28,32},{32,36}... | collective-permute-start | bytes 2359304 | tf_op jit(solution)/shard_map/while/body/eval_jaxpr/ppermute | solution.py:28
  879.9 15.5 %collective-permute-start.4 = (f32[3,32,16,128]{3,1,2,0:T(8,128)S(1)}, f32[3,32,16,128]{3,1,2,0:T(8,128)}, u32[]{:S(2)}, u32[]{:S(2)}) collective-permute-start(f32[3,32,16,128]{3,1,2,0:T(8,128)S(1)} %fusion.95), channel_id=1, source_target_pairs={{0,4},{4,8},{8,12},{12,16},{16,20},{20,24},{24,28},{28,32},{32,36}... | collective-permute-start | bytes 2359304 | tf_op jit(solution)/shard_map/while/body/eval_jaxpr/ppermute | solution.py:28
  917.1 15.5 %collective-permute-start.4 = (f32[3,32,16,128]{3,1,2,0:T(8,128)S(1)}, f32[3,32,16,128]{3,1,2,0:T(8,128)}, u32[]{:S(2)}, u32[]{:S(2)}) collective-permute-start(f32[3,32,16,128]{3,1,2,0:T(8,128)S(1)} %fusion.95), channel_id=1, source_target_pairs={{0,4},{4,8},{8,12},{12,16},{16,20},{20,24},{24,28},{28,32},{32,36}... | collective-permute-start | bytes 2359304 | tf_op jit(solution)/shard_map/while/body/eval_jaxpr/ppermute | solution.py:28
  954.3 15.5 %collective-permute-start.4 = (f32[3,32,16,128]{3,1,2,0:T(8,128)S(1)}, f32[3,32,16,128]{3,1,2,0:T(8,128)}, u32[]{:S(2)}, u32[]{:S(2)}) collective-permute-start(f32[3,32,16,128]{3,1,2,0:T(8,128)S(1)} %fusion.95), channel_id=1, source_target_pairs={{0,4},{4,8},{8,12},{12,16},{16,20},{20,24},{24,28},{28,32},{32,36}... | collective-permute-start | bytes 2359304 | tf_op jit(solution)/shard_map/while/body/eval_jaxpr/ppermute | solution.py:28
  991.5 15.5 %collective-permute-start.4 = (f32[3,32,16,128]{3,1,2,0:T(8,128)S(1)}, f32[3,32,16,128]{3,1,2,0:T(8,128)}, u32[]{:S(2)}, u32[]{:S(2)}) collective-permute-start(f32[3,32,16,128]{3,1,2,0:T(8,128)S(1)} %fusion.95), channel_id=1, source_target_pairs={{0,4},{4,8},{8,12},{12,16},{16,20},{20,24},{24,28},{28,32},{32,36}... | collective-permute-start | bytes 2359304 | tf_op jit(solution)/shard_map/while/body/eval_jaxpr/ppermute | solution.py:28
  1028.7 15.5 %collective-permute-start.4 = (f32[3,32,16,128]{3,1,2,0:T(8,128)S(1)}, f32[3,32,16,128]{3,1,2,0:T(8,128)}, u32[]{:S(2)}, u32[]{:S(2)}) collective-permute-start(f32[3,32,16,128]{3,1,2,0:T(8,128)S(1)} %fusion.95), channel_id=1, source_target_pairs={{0,4},{4,8},{8,12},{12,16},{16,20},{20,24},{24,28},{28,32},{32,36}... | collective-permute-start | bytes 2359304 | tf_op jit(solution)/shard_map/while/body/eval_jaxpr/ppermute | solution.py:28
  1066.0 15.5 %collective-permute-start.4 = (f32[3,32,16,128]{3,1,2,0:T(8,128)S(1)}, f32[3,32,16,128]{3,1,2,0:T(8,128)}, u32[]{:S(2)}, u32[]{:S(2)}) collective-permute-start(f32[3,32,16,128]{3,1,2,0:T(8,128)S(1)} %fusion.95), channel_id=1, source_target_pairs={{0,4},{4,8},{8,12},{12,16},{16,20},{20,24},{24,28},{28,32},{32,36}... | collective-permute-start | bytes 2359304 | tf_op jit(solution)/shard_map/while/body/eval_jaxpr/ppermute | solution.py:28
  1103.2 15.5 %collective-permute-start.4 = (f32[3,32,16,128]{3,1,2,0:T(8,128)S(1)}, f32[3,32,16,128]{3,1,2,0:T(8,128)}, u32[]{:S(2)}, u32[]{:S(2)}) collective-permute-start(f32[3,32,16,128]{3,1,2,0:T(8,128)S(1)} %fusion.95), channel_id=1, source_target_pairs={{0,4},{4,8},{8,12},{12,16},{16,20},{20,24},{24,28},{28,32},{32,36}... | collective-permute-start | bytes 2359304 | tf_op jit(solution)/shard_map/while/body/eval_jaxpr/ppermute | solution.py:28
  1140.4 15.5 %collective-permute-start.4 = (f32[3,32,16,128]{3,1,2,0:T(8,128)S(1)}, f32[3,32,16,128]{3,1,2,0:T(8,128)}, u32[]{:S(2)}, u32[]{:S(2)}) collective-permute-start(f32[3,32,16,128]{3,1,2,0:T(8,128)S(1)} %fusion.95), channel_id=1, source_target_pairs={{0,4},{4,8},{8,12},{12,16},{16,20},{20,24},{24,28},{28,32},{32,36}... | collective-permute-start | bytes 2359304 | tf_op jit(solution)/shard_map/while/body/eval_jaxpr/ppermute | solution.py:28
  1177.6 15.5 %collective-permute-start.4 = (f32[3,32,16,128]{3,1,2,0:T(8,128)S(1)}, f32[3,32,16,128]{3,1,2,0:T(8,128)}, u32[]{:S(2)}, u32[]{:S(2)}) collective-permute-start(f32[3,32,16,128]{3,1,2,0:T(8,128)S(1)} %fusion.95), channel_id=1, source_target_pairs={{0,4},{4,8},{8,12},{12,16},{16,20},{20,24},{24,28},{28,32},{32,36}... | collective-permute-start | bytes 2359304 | tf_op jit(solution)/shard_map/while/body/eval_jaxpr/ppermute | solution.py:28
  1214.8 15.5 %collective-permute-start.4 = (f32[3,32,16,128]{3,1,2,0:T(8,128)S(1)}, f32[3,32,16,128]{3,1,2,0:T(8,128)}, u32[]{:S(2)}, u32[]{:S(2)}) collective-permute-start(f32[3,32,16,128]{3,1,2,0:T(8,128)S(1)} %fusion.95), channel_id=1, source_target_pairs={{0,4},{4,8},{8,12},{12,16},{16,20},{20,24},{24,28},{28,32},{32,36}... | collective-permute-start | bytes 2359304 | tf_op jit(solution)/shard_map/while/body/eval_jaxpr/ppermute | solution.py:28
  1252.0 15.5 %collective-permute-start.4 = (f32[3,32,16,128]{3,1,2,0:T(8,128)S(1)}, f32[3,32,16,128]{3,1,2,0:T(8,128)}, u32[]{:S(2)}, u32[]{:S(2)}) collective-permute-start(f32[3,32,16,128]{3,1,2,0:T(8,128)S(1)} %fusion.95), channel_id=1, source_target_pairs={{0,4},{4,8},{8,12},{12,16},{16,20},{20,24},{24,28},{28,32},{32,36}... | collective-permute-start | bytes 2359304 | tf_op jit(solution)/shard_map/while/body/eval_jaxpr/ppermute | solution.py:28
  (158 other events, 1019.7 us)
where the time goes:
time: 1280 us; the launch traced here: 1270 us
  waiting for transfers between devices  694 us (54%)
  starting transfers between devices  300 us (23%)
  other arithmetic  137 us (11%)
  local copies, waits for them, and re-layouts  76.3 us (6%)
  matrix products  58.2 us (5%)
    ppermute x33, waiting for transfers between devices, passed_along(): return lax.ppermute(value, axis, pairs)  404 us
    ppermute x68, waiting for transfers between devices, extended_2(): lax.ppermute(lax.slice_in_dim(block, block.shape[dim] - width, None, axis...  270 us
    ppermute x68, starting transfers between devices, extended_2(): lax.ppermute(lax.slice_in_dim(block, 0, width, axis=dim), axis, backward)  148 us
    ppermute x68, starting transfers between devices, extended_2(): lax.ppermute(lax.slice_in_dim(block, block.shape[dim] - width, None, axis...  87.9 us
    ppermute x33, starting transfers between devices, passed_along(): return lax.ppermute(value, axis, pairs)  63.4 us
    dot_general x68, matrix products, convolve(): jnp.einsum('iok,inkrw->inorw', matrices, patches, preferred_element_type=...  58.2 us
    while x384, local copies, waits for them, and re-layouts  47.1 us
    another operation x32, other arithmetic, advance(): return jnp.stack(results)  43.7 us
  transfers between devices with their start and end apart: 169, of which 168 were waited for; matrix products, arithmetic and copies ran while one was open for 3% of the time, Pallas kernels for 0%

commit v1 on v0

v1 whole, which is shorter than its diff:
```python
import functools

import jax
import jax.numpy as jnp
from jax import lax
from jax.experimental import pallas as pl
from jax.experimental.pallas import tpu as pltpu
from jax.sharding import PartitionSpec as P

M = 4
H = 0.125
C = 32
W = 128
BAND = 16
SUB = 8
STEPS = 2 * SUB
IMAGES = 3
WIN = 3 * BAND
REACH = 4
SPAN = BAND + 2 * REACH
PHASE = [BAND - 4 * q for q in range(4)]
OFFSET = [4 * sum(PHASE[:q]) for q in range(4)]
HALO = 4 * sum(PHASE)
CHUNK = 2 * BAND + 6
bf16 = jnp.bfloat16
f32 = jnp.float32


def home(b):
    return 2 * b


def taps(weights):
    n = weights.shape[0]
    w = weights.reshape(n, C, 3, 3, C).transpose(0, 3, 1, 2, 4).reshape(n, 3, C, 3 * C)
    return jnp.pad(w, ((0, 0), (0, 0), (0, 0), (0, W - 3 * C)))


def banded(tap):
    columns = []
    for dc in range(3):
        top = tap[dc]
        low = pltpu.roll(top.astype(f32), C, 1).astype(bf16)
        columns.append(jnp.concatenate([top, low], axis=0))
    return jnp.concatenate(columns, axis=1)


def spread(xs, buf, row, value):
    lane = lax.broadcasted_iota(jnp.int32, (2 * C, W), 1)
    left = jnp.where(lane == 0, 0.0, pltpu.roll(value, 1, 1))
    right = jnp.where(lane == W - 1, 0.0, pltpu.roll(value, W - 1, 1))
    for dc, v in enumerate((left, value, right)):
        xs[buf, dc, row : row + 2] = v.astype(bf16).reshape(2, C, W)


def block(xs, buf, matrix, row):
    parts = []
    for dc in range(3):
        a = xs[buf, dc, row : row + 4].reshape(4 * C, W)
        b = xs[buf, dc, row + 2 : row + 6].reshape(4 * C, W)
        parts.append(jnp.concatenate([a, b], axis=1))
    rhs = jnp.concatenate(parts, axis=0)
    z = jnp.dot(matrix, rhs, preferred_element_type=f32)
    return jnp.tanh(z[:, :W]), jnp.tanh(z[:, W:])


def clear_rims(xs, rows):
    for buf in range(2):
        for dc in range(3):
            for row in (0, rows + 1):
                xs[buf, dc, row] = jnp.zeros((C, W), bf16)


def relax_kernel(z_ref, own_ref, up_ref, dn_ref, img_ref, tap_ref, out_ref, v1_ref, xs, state, base):
    z = z_ref[0]
    clear_rims(xs, SPAN)
    low_ok = jnp.where(z > 0, 1.0, 0.0)
    high_ok = jnp.where(z < 3, 1.0, 0.0)

    def put(buf, pair, value):
        if pair < REACH // 2:
            value = value * low_ok
        elif pair >= (REACH + BAND) // 2:
            value = value * high_ok
        spread(xs, buf, 2 * pair + 1, value)

    def unit(u, carry):
        for pair in range(SPAN // 2):
            r = 2 * pair
            if r < REACH:
                x = up_ref[u, r : r + 2]
            elif r < REACH + BAND:
                x = own_ref[u, r - REACH : r - REACH + 2]
            else:
                x = dn_ref[u, r - REACH - BAND : r - REACH - BAND + 2]
            x = x.astype(f32).reshape(2 * C, W)
            state[r : r + 2] = x.reshape(2, C, W)
            put(0, pair, x)
        first = 4 * jnp.where(u == 2 * IMAGES, 2, u // IMAGES)
        for j in range(M):
            matrix = banded(tap_ref[first + j])
            for q in range(SPAN // 4):
                pair_t = block(xs, j % 2, matrix, 4 * q)
                for i, t in enumerate(pair_t):
                    r = 4 * q + 2 * i
                    x = state[r : r + 2].reshape(2 * C, W)
                    if j == 0 and REACH <= r < REACH + BAND:
                        base[r - REACH : r - REACH + 2] = (x + (M * H) * t).reshape(2, C, W)
                    x = x + H * t
                    state[r : r + 2] = x.reshape(2, C, W)
                    if j < M - 1:
                        put((j + 1) % 2, r // 2, x)

        @pl.when(u < 2 * IMAGES)
        def _():
            point, b = u // IMAGES, lax.rem(u, IMAGES)
            out_ref[b, pl.ds(point * BAND, BAND)] = (state[REACH : REACH + BAND] - base[...]).astype(bf16)

        @pl.when(u == 2 * IMAGES)
        def _():
            v1_ref[...] = img_ref[...] + (state[REACH : REACH + BAND] - own_ref[2 * IMAGES].astype(f32))

        return carry

    lax.fori_loop(0, 2 * IMAGES + 1, unit, 0)
    for b in range(IMAGES):
        out_ref[b, 2 * BAND : 2 * BAND + 3] = tap_ref[0]
        out_ref[b, 2 * BAND + 3 : 2 * BAND + 6] = tap_ref[4]


def pack_kernel(sub_ref, *refs):
    chunks, v1_ref, d_ref, w_ref, up_ref, dn_ref = refs[:SUB], refs[SUB], *refs[SUB + 1 :]
    sub = sub_ref[0]
    for r in range(SUB):
        at = lax.rem(sub + r, SUB)
        for p in range(2):
            d_ref[2 * at + p] = chunks[r][p * BAND : (p + 1) * BAND]
            w_ref[2 * at + p] = chunks[r][2 * BAND + 3 * p : 2 * BAND + 3 * p + 3]
    for q, rows in enumerate(PHASE):
        for s in range(4):
            to = OFFSET[q] + s * rows
            up_ref[to : to + rows] = d_ref[4 * q + s, BAND - rows :]
            dn_ref[to : to + rows] = d_ref[4 * q + s, :rows]
    v1 = v1_ref[...].astype(bf16)
    up_ref[HALO:] = v1
    dn_ref[HALO:] = v1


def sweep_kernel(
    info_ref, v1_ref, own_ref, above_ref, below_ref, d_ref, up_ref, dn_ref, w_ref,
    res_ref, out_ref, edge_ref, xs, state,
):
    z, sub, first = info_ref[0], info_ref[1], info_ref[2]
    clear_rims(xs, WIN)
    low_ok = jnp.where(z > 0, 1.0, 0.0)
    high_ok = jnp.where(z < 3, 1.0, 0.0)

    def put(buf, row, value):
        if row < BAND:
            value = value * low_ok
        elif row >= 2 * BAND:
            value = value * high_ok
        spread(xs, buf, row + 1, value)

    @pl.when(first == 1)
    def _():
        state[:BAND] = up_ref[HALO:].astype(f32)
        state[BAND : 2 * BAND] = v1_ref[...]
        state[2 * BAND :] = dn_ref[HALO:].astype(f32)

    @pl.when(first == 0)
    def _():
        state[:BAND] = above_ref[...].astype(f32)
        state[BAND : 2 * BAND] = own_ref[...]
        state[2 * BAND :] = below_ref[...].astype(f32)

    for row in range(0, WIN, 2):
        put(0, row, state[row : row + 2].reshape(2 * C, W))

    for q, rows in enumerate(PHASE):

        def step(i, carry, q=q, rows=rows):
            s = 4 * q + i
            now, later = lax.rem(s, 2), lax.rem(s + 1, 2)
            matrix = banded(w_ref[s])
            res_ref[lax.rem(s // 2 - sub + SUB, SUB), lax.rem(s, 2)] = xs[now, 1, BAND + 1 : 2 * BAND + 1]
            for row in range(BAND - rows, 2 * BAND + rows, 4):
                for k, t in enumerate(block(xs, now, matrix, row)):
                    r = row + 2 * k
                    if r < BAND:
                        at = OFFSET[q] + i * rows + (r - (BAND - rows))
                        d = up_ref[pl.ds(at, 2)]
                    elif r < 2 * BAND:
                        d = d_ref[s, r - BAND : r - BAND + 2]
                    else:
                        at = OFFSET[q] + i * rows + (r - 2 * BAND)
                        d = dn_ref[pl.ds(at, 2)]
                    x = state[r : r + 2].reshape(2 * C, W) + (M * H) * t + d.astype(f32).reshape(2 * C, W)
                    state[r : r + 2] = x.reshape(2, C, W)
                    put(later, r, x)
            return carry

        lax.fori_loop(0, 4, step, 0)
    out_ref[...] = state[BAND : 2 * BAND]
    edge_ref[...] = state[BAND : 2 * BAND].astype(bf16)


VM = pl.BlockSpec(memory_space=pltpu.VMEM)
SM = pl.BlockSpec(memory_space=pltpu.SMEM)


def shape(*dims, dtype=bf16):
    return jax.ShapeDtypeStruct(dims, dtype)


def relax(z, own, up, dn, image, tap):
    return pl.pallas_call(
        relax_kernel,
        out_shape=(shape(IMAGES, CHUNK, C, W), shape(BAND, C, W, dtype=f32)),
        in_specs=[SM] + [VM] * 5,
        out_specs=(VM, VM),
        scratch_shapes=[
            pltpu.VMEM((2, 3, SPAN + 2, C, W), bf16),
            pltpu.VMEM((SPAN, C, W), f32),
            pltpu.VMEM((BAND, C, W), f32),
        ],
        name="relax",
    )(z, own, up, dn, image, tap)


def pack(sub, chunks, v1):
    return pl.pallas_call(
        pack_kernel,
        out_shape=(
            shape(STEPS, BAND, C, W),
            shape(STEPS, 3, C, W),
            shape(HALO + BAND, C, W),
            shape(HALO + BAND, C, W),
        ),
        in_specs=[SM] + [VM] * (SUB + 1),
        out_specs=(VM,) * 4,
        name="pack",
    )(sub, *chunks, v1)


def sweep(info, *arrays):
    return pl.pallas_call(
        sweep_kernel,
        out_shape=(shape(SUB, 2, BAND, C, W), shape(BAND, C, W, dtype=f32), shape(BAND, C, W)),
        in_specs=[SM] + [VM] * 8,
        out_specs=(VM,) * 3,
        scratch_shapes=[
            pltpu.VMEM((2, 3, WIN + 2, C, W), bf16),
            pltpu.VMEM((WIN, C, W), f32),
        ],
        name="sweep",
    )(info, *arrays)


def per_device(weights, image, guess):
    layers, rows = lax.axis_size("layer"), lax.axis_size("rows")
    groups = layers // SUB
    l, z = lax.axis_index("layer"), lax.axis_index("rows")
    sub, group = lax.rem(l, SUB), l // SUB
    mine = jnp.minimum(sub // 2, IMAGES - 1)

    tap = taps(weights)
    following = lax.ppermute(tap[:M], "layer", [(i + 1, i) for i in range(layers - 1)])
    opening = tap[:M]
    for b in range(1, IMAGES):
        got = lax.ppermute(tap[:M], "layer", [(0, home(b))])
        opening = jnp.where(l == home(b), got, opening)
    tap = jnp.concatenate([tap[M:], following, opening], axis=0)

    own_image = lax.dynamic_index_in_dim(image, mine, 0, keepdims=False).transpose(1, 0, 2)
    points = guess.reshape(2 * IMAGES, C, BAND, W).transpose(0, 2, 1, 3).astype(bf16)
    points = jnp.concatenate([points, own_image.astype(bf16)[None]], axis=0)
    up = lax.ppermute(points[:, BAND - REACH :], "rows", [(i, i + 1) for i in range(rows - 1)])
    dn = lax.ppermute(points[:, :REACH], "rows", [(i + 1, i) for i in range(rows - 1)])

    zs = z.astype(jnp.int32).reshape(1)
    chunk, v1 = relax(zs, points, up, dn, own_image, tap)

    received = [lax.dynamic_index_in_dim(chunk, mine, 0, keepdims=False)]
    for r in range(1, SUB):
        target = jnp.clip(lax.rem(sub - r + SUB, SUB) // 2, 0, IMAGES - 1)
        value = lax.dynamic_index_in_dim(chunk, target, 0, keepdims=False)
        pairs = [
            (SUB * g + (home(b) + r) % SUB, SUB * g + home(b)) for g in range(groups) for b in range(IMAGES)
        ]
        received.append(lax.ppermute(value, "layer", pairs))
    d, w, up, dn = pack(sub.astype(jnp.int32).reshape(1), received, v1)
    above = lax.ppermute(up, "rows", [(i, i + 1) for i in range(rows - 1)])
    below = lax.ppermute(dn, "rows", [(i + 1, i) for i in range(rows - 1)])

    info = jnp.stack([z, sub, jnp.where(group == 0, 1, 0)]).astype(jnp.int32)
    def handoff(value, by):
        pairs = []
        for g in range(groups - 1):
            for b in range(IMAGES):
                for k in range(rows):
                    if 0 <= k + by < rows:
                        source = (SUB * g + home(b)) * rows + k
                        target = (SUB * (g + 1) + home(b)) * rows + k + by
                        pairs.append((source, target))
        return lax.ppermute(value, ("layer", "rows"), pairs)

    state, low, high = v1, above[HALO:], below[HALO:]
    for stage in range(groups):
        results, state, edge = sweep(info, v1, state, low, high, d, above, below, w)
        if stage < groups - 1:
            state, low, high = handoff(state, 0), handoff(edge, 1), handoff(edge, -1)

    slots = [results[0]]
    for r in range(1, SUB):
        pairs = [
            (SUB * g + home(b), SUB * g + (home(b) + r) % SUB) for g in range(groups) for b in range(IMAGES)
        ]
        slots.append(lax.ppermute(results[r], "layer", pairs))
    slots = jnp.stack(slots)
    images = [
        lax.dynamic_index_in_dim(slots, lax.rem(sub - home(b) + SUB, SUB), 0, keepdims=False)
        for b in range(IMAGES)
    ]
    return jnp.stack(images, axis=1).transpose(0, 1, 3, 2, 4).astype(f32)


def solution(mesh):
    return jax.shard_map(
        per_device,
        mesh=mesh,
        in_specs=(
            P("layer", None, None),
            P(None, None, "rows", None),
            P("layer", None, None, "rows", None),
        ),
        out_specs=P("layer", None, None, "rows", None),
        check_vma=False,
    )
```

time: 1280 us -> 351 us (0.27)
  waiting for transfers between devices: 694 us -> 69.9 us
  starting transfers between devices: 300 us -> 61.2 us
  Pallas kernels: 0 us -> 190 us
  other arithmetic: 137 us -> 4.19 us
  matrix products: 58.2 us -> 0 us
  local copies, waits for them, and re-layouts: 76.3 us -> 21.6 us
    ppermute x169 -> x30, waiting for transfers between devices: 694 us -> 69.9 us  [the longest x1 24.5 us: per_device(): above = lax.ppermute(up, 'rows', [(i, i + 1) for i in range(rows - 1)])]
    ppermute x169 -> x30, starting transfers between devices: 300 us -> 61.2 us  [the longest x9 17 us: handoff(): return lax.ppermute(value, ('layer', 'rows'), pairs)]
    pallas_call x0 -> x6, Pallas kernels: none -> 190 us  [the longest x4 173 us: sweep(): pl.pallas_call(sweep_kernel, out_shape=(shape(SUB, 2, BAND, C, W), shape(...]
    dot_general x68 -> x0, matrix products: 58.2 us -> none  [convolve(): jnp.einsum('iok,inkrw->inorw', matrices, patches, preferred_element_type=...]
    while x385 -> x0, local copies, waits for them, and re-layouts: 50.5 us -> none
    another operation x32 -> x1, other arithmetic: 43.7 us -> 0.65 us  [per_device(): info = jnp.stack([z, sub, jnp.where(group == 0, 1, 0)]).astype(jnp.int32)]
    select_n x32 -> x0, other arithmetic: 40.8 us -> none  [sweep(): return (jnp.where(section == 0, image, sent), fresh)]
    concatenate x68 -> x3, other arithmetic: 32.3 us -> 1.84 us  [the longest x2 1.08 us: per_device(): points = jnp.concatenate([points, own_image.astype(bf16)[None]], axis=0)]
  transfers between devices with their start and end apart: 169 -> 30, of which waited for: 168 -> 14; matrix products, arithmetic and copies ran while one was open for 3% -> 2% of each run, Pallas kernels for 0% -> 0%
where the time goes in v1:
time: 351 us; the launch traced here: 347 us
  Pallas kernels  190 us (54%)
  waiting for transfers between devices  69.9 us (20%)
  starting transfers between devices  61.2 us (17%)
  local copies, waits for them, and re-layouts  21.6 us (6%)
  other arithmetic  4.19 us (1%)
    pallas_call x4, Pallas kernels, sweep(): pl.pallas_call(sweep_kernel, out_shape=(shape(SUB, 2, BAND, C, W), shape(...  173 us
    ppermute x1, waiting for transfers between devices, per_device(): above = lax.ppermute(up, 'rows', [(i, i + 1) for i in range(rows - 1)])  24.5 us
    ppermute x9, waiting for transfers between devices, handoff(): return lax.ppermute(value, ('layer', 'rows'), pairs)  21.3 us
    ppermute x9, starting transfers between devices, handoff(): return lax.ppermute(value, ('layer', 'rows'), pairs)  17 us
    ppermute x7, starting transfers between devices, per_device(): slots.append(lax.ppermute(results[r], 'layer', pairs))  15.8 us
    ppermute x7, waiting for transfers between devices, per_device(): received.append(lax.ppermute(value, 'layer', pairs))  14.1 us
    pallas_call x1, Pallas kernels, relax(): pl.pallas_call(relax_kernel, out_shape=(shape(IMAGES, CHUNK, C, W), shape...  12.4 us
    ppermute x7, starting transfers between devices, per_device(): received.append(lax.ppermute(value, 'layer', pairs))  12.1 us
  transfers between devices with their start and end apart: 30, of which 14 were waited for; matrix products, arithmetic and copies ran while one was open for 2% of the time, Pallas kernels for 0%

profile of v1, /device:TPU:100, one launch (start us, length us, event | category | flops | bytes accessed | tf_op | source)
XLA Modules:
  0.0 347.4 jit_solution(4944710061366730531)
XLA Ops:
  0.0 1.7 reshape.13
  3.9 4.3 %collective-permute-start.2 = (bf16[4,3,32,128]{3,2,1,0:T(8,128)(2,1)S(1)}, bf16[4,3,32,128]{3,2,1,0:T(8,128)(2,1)S(1)}, u32[]{:S(2)}, u32[]{:S(2)}) collective-permute-start(bf16[4,3,32,128]{3,2,1,0:T(8,128)(2,1)S(1)} %pad_slice_fusion.4), channel_id=1, source_target_pairs={{4,0},{8,4},{12,8},{16,12},{20,16},{24,20},{28,24},{32,28},{36,32}... | collective-permute-start | bytes 294920 | tf_op jit(solution)/shard_map/ppermute | solution.py:268
  8.4 1.5 convert_element_type.20
  10.2 2.3 collective-permute-start.1
  12.5 1.3 collective-permute-start
  16.6 3.8 %collective-permute-done.up_ref = bf16[7,4,32,128]{3,2,1,0:T(8,128)(2,1)S(1)} collective-permute-done((bf16[7,4,32,128]{3,2,1,0:T(8,128)(2,1)S(1)}, bf16[7,4,32,128]{3,2,1,0:T(8,128)(2,1)S(1)}, u32[]{:S(2)}, u32[]{:S(2)}) %collective-permute-start) | collective-permute-done | bytes 229408 | tf_op jit(solution)/shard_map/ppermute | solution.py:278
  21.1 12.4 %relax.1 = (bf16[3,38,32,128]{3,2,1,0:T(8,128)(2,1)}, f32[16,32,128]{2,1,0:T(8,128)}) custom-call(s32[1]{0:T(128)} %bitcast.z_ref, bf16[7,16,32,128]{3,2,1,0:T(8,128)(2,1)} %pad_maximum_fusion.own_ref, bf16[7,4,32,128]{3,2,1,0:T(8,128)(2,1)} %copy-done.13, bf16[7,4,32,128]{3,2,1,0:T(8,128)(2,1)} %copy-done.12, f32[16,32,128]{2,1,0:T(8,128)} %bitcast.75, ...), custom_call_target="tpu_custom_call" | custom-call | tf_op jit(solution)/shard_map/relax/pallas_call | solution.py:217
  33.5 3.0 dynamic-slice_bitcast_fusion
  37.8 2.8 collective-permute-start.10
  40.6 1.3 collective-permute-start.9
  41.9 2.9 collective-permute-start.8
  44.8 1.3 collective-permute-start.7
  46.1 7.9 %collective-permute-done.11.refs_7_ = bf16[38,32,128]{2,1,0:T(8,128)(2,1)S(1)} collective-permute-done((bf16[38,32,128]{2,1,0:T(8,128)(2,1)S(1)}, bf16[38,32,128]{2,1,0:T(8,128)(2,1)S(1)}, u32[]{:S(2)}, u32[]{:S(2)}) %collective-permute-start.11) | collective-permute-done | bytes 311328 | tf_op jit(solution)/shard_map/ppermute | solution.py:291
  54.1 1.3 collective-permute-start.6
  57.3 5.6 %collective-permute-done.6.refs_2_ = bf16[38,32,128]{2,1,0:T(8,128)(2,1)S(1)} collective-permute-done((bf16[38,32,128]{2,1,0:T(8,128)(2,1)S(1)}, bf16[38,32,128]{2,1,0:T(8,128)(2,1)S(1)}, u32[]{:S(2)}, u32[]{:S(2)}) %collective-permute-start.6) | collective-permute-done | bytes 311328 | tf_op jit(solution)/shard_map/ppermute | solution.py:291
  63.7 4.1 %pack.1 = (bf16[16,16,32,128]{3,2,1,0:T(8,128)(2,1)}, bf16[16,3,32,128]{3,2,1,0:T(8,128)(2,1)}, bf16[176,32,128]{2,1,0:T(8,128)(2,1)}, bf16[176,32,128]{2,1,0:T(8,128)(2,1)}) custom-call(s32[1]{0:T(128)} %bitcast.1.sub_ref, bf16[38,32,128]{2,1,0:T(8,128)(2,1)} %get-tuple-element.49.refs_0_, bf16[38,32,128]{2,1,0:T(8,128)(2,1)} %copy-done.8, ...), custom_call_target="tpu_custom_call" | custom-call | tf_op jit(solution)/shard_map/pack/pallas_call | solution.py:232
  69.2 5.7 %collective-permute-start.13 = (bf16[176,32,128]{2,1,0:T(8,128)(2,1)}, bf16[176,32,128]{2,1,0:T(8,128)(2,1)}, u32[]{:S(2)}, u32[]{:S(2)}) collective-permute-start(bf16[176,32,128]{2,1,0:T(8,128)(2,1)} %get-tuple-element.21), channel_id=1, source_target_pairs={{1,0},{2,1},{3,2},{5,4},{6,5},{7,6},{9,8},{10,9},{11,10},{13,12},{... | collective-permute-start | bytes 4325384 | tf_op jit(solution)/shard_map/ppermute | solution.py:294
  75.5 24.5 %collective-permute-done.12.up_ref = bf16[176,32,128]{2,1,0:T(8,128)(2,1)S(1)} collective-permute-done((bf16[176,32,128]{2,1,0:T(8,128)(2,1)}, bf16[176,32,128]{2,1,0:T(8,128)(2,1)S(1)}, u32[]{:S(2)}, u32[]{:S(2)}) %collective-permute-start.12) | collective-permute-done | bytes 1441824 | tf_op jit(solution)/shard_map/ppermute | solution.py:293
  101.3 1.6 slice.64.below_ref
  102.9 43.3 %sweep.4 = (bf16[8,2,16,32,128]{4,3,2,1,0:T(8,128)(2,1)}, f32[16,32,128]{2,1,0:T(8,128)}, bf16[16,32,128]{2,1,0:T(8,128)(2,1)}) custom-call(s32[3]{0:T(128)} %pad_add_fusion.info_ref, f32[16,32,128]{2,1,0:T(8,128)} %get-tuple-element.18.refs_8_.v1_ref.own_ref, f32[16,32,128]{2,1,0:T(8,128)} %get-tuple-element.18.refs_8_.v1_ref.own_ref, ...), custom_call_target="tpu_custom_call" | custom-call | tf_op jit(solution)/shard_map/sweep/pallas_call | solution.py:247
  146.2 3.4 collective-permute-start.14
  149.6 3.2 collective-permute-start.16
  152.8 1.3 collective-permute-start.15
  154.1 1.5 collective-permute-done.16.below_ref
  155.6 5.2 %collective-permute-done.15.above_ref = bf16[16,32,128]{2,1,0:T(8,128)(2,1)S(1)} collective-permute-done((bf16[16,32,128]{2,1,0:T(8,128)(2,1)}, bf16[16,32,128]{2,1,0:T(8,128)(2,1)S(1)}, u32[]{:S(2)}, u32[]{:S(2)}) %collective-permute-start.15) | collective-permute-done | bytes 131104 | tf_op jit(solution)/shard_map/ppermute | solution.py:306
  162.2 43.5 %sweep.5 = (bf16[8,2,16,32,128]{4,3,2,1,0:T(8,128)(2,1)}, f32[16,32,128]{2,1,0:T(8,128)}, bf16[16,32,128]{2,1,0:T(8,128)(2,1)}) custom-call(s32[3]{0:T(128)} %pad_add_fusion.info_ref, f32[16,32,128]{2,1,0:T(8,128)} %get-tuple-element.18.refs_8_.v1_ref.own_ref, f32[16,32,128]{2,1,0:T(8,128)} %copy-done.10, bf16[16,32,128]{2,1,0:T(8,128)(2,1)} %copy-done.18, ...), custom_call_target="tpu_custom_call" | custom-call | tf_op jit(solution)/shard_map/sweep/pallas_call | solution.py:247
  205.6 2.0 collective-permute-start.17
  207.6 1.3 collective-permute-start.19
  208.9 1.3 collective-permute-start.18
  210.2 3.0 collective-permute-done.19.below_ref
  213.2 4.3 %collective-permute-done.18.above_ref = bf16[16,32,128]{2,1,0:T(8,128)(2,1)S(1)} collective-permute-done((bf16[16,32,128]{2,1,0:T(8,128)(2,1)}, bf16[16,32,128]{2,1,0:T(8,128)(2,1)S(1)}, u32[]{:S(2)}, u32[]{:S(2)}) %collective-permute-start.18) | collective-permute-done | bytes 131104 | tf_op jit(solution)/shard_map/ppermute | solution.py:306
  218.9 43.3 %sweep.6 = (bf16[8,2,16,32,128]{4,3,2,1,0:T(8,128)(2,1)}, f32[16,32,128]{2,1,0:T(8,128)}, bf16[16,32,128]{2,1,0:T(8,128)(2,1)}) custom-call(s32[3]{0:T(128)} %pad_add_fusion.info_ref, f32[16,32,128]{2,1,0:T(8,128)} %get-tuple-element.18.refs_8_.v1_ref.own_ref, f32[16,32,128]{2,1,0:T(8,128)} %copy-done.11, bf16[16,32,128]{2,1,0:T(8,128)(2,1)} %copy-done.19, ...), custom_call_target="tpu_custom_call" | custom-call | tf_op jit(solution)/shard_map/sweep/pallas_call | solution.py:247
  262.2 1.9 collective-permute-start.20
  264.1 1.3 collective-permute-start.22
  265.4 1.3 collective-permute-start.21
  266.7 3.0 collective-permute-done.22.below_ref
  269.7 4.3 %collective-permute-done.21.above_ref = bf16[16,32,128]{2,1,0:T(8,128)(2,1)S(1)} collective-permute-done((bf16[16,32,128]{2,1,0:T(8,128)(2,1)}, bf16[16,32,128]{2,1,0:T(8,128)(2,1)S(1)}, u32[]{:S(2)}, u32[]{:S(2)}) %collective-permute-start.21) | collective-permute-done | bytes 131104 | tf_op jit(solution)/shard_map/ppermute | solution.py:306
  275.4 43.2 %sweep.7 = (bf16[8,2,16,32,128]{4,3,2,1,0:T(8,128)(2,1)}, f32[16,32,128]{2,1,0:T(8,128)}, bf16[16,32,128]{2,1,0:T(8,128)(2,1)}) custom-call(s32[3]{0:T(128)} %pad_add_fusion.info_ref, f32[16,32,128]{2,1,0:T(8,128)} %get-tuple-element.18.refs_8_.v1_ref.own_ref, f32[16,32,128]{2,1,0:T(8,128)} %copy-done.9, bf16[16,32,128]{2,1,0:T(8,128)(2,1)} %copy-done.15, ...), custom_call_target="tpu_custom_call" | custom-call | tf_op jit(solution)/shard_map/sweep/pallas_call | solution.py:247
  318.6 2.9 slice_bitcast_fusion
  321.5 2.0 collective-permute-start.23
  323.5 4.7 %collective-permute-start.24 = (bf16[2,16,32,128]{3,2,1,0:T(8,128)(2,1)}, bf16[2,16,32,128]{3,2,1,0:T(8,128)(2,1)}, u32[]{:S(2)}, u32[]{:S(2)}) collective-permute-start(bf16[2,16,32,128]{3,2,1,0:T(8,128)(2,1)} %get-tuple-element.39), channel_id=1, source_target_pairs={{0,8},{8,16},{16,24},{32,40},{40,48},{48,56},{64,72},{72,80},{80,8... | collective-permute-start | bytes 786440 | tf_op jit(solution)/shard_map/ppermute | solution.py:319
  328.1 1.3 collective-permute-start.29
  329.4 1.9 collective-permute-start.28
  331.4 1.3 collective-permute-start.27
  332.7 1.3 collective-permute-start.25
  335.0 3.3 collective-permute-start.26
  339.7 5.3 %collective-permute-done.26 = bf16[2,16,32,128]{3,2,1,0:T(8,128)(2,1)S(1)} collective-permute-done((bf16[2,16,32,128]{3,2,1,0:T(8,128)(2,1)}, bf16[2,16,32,128]{3,2,1,0:T(8,128)(2,1)S(1)}, u32[]{:S(2)}, u32[]{:S(2)}) %collective-permute-start.26) | collective-permute-done | bytes 262176 | tf_op jit(solution)/shard_map/ppermute | solution.py:319
  345.4 2.0 copy.10
  (86 shorter events, 19.8 us)
Async XLA Ops:
  0.0 8.3 %copy-start = (f32[3,32,16,128]{3,2,1,0:T(8,128)S(1)}, f32[3,32,16,128]{3,2,1,0:T(8,128)}, u32[]{:S(2)}) copy-start(f32[3,32,16,128]{3,2,1,0:T(8,128)} %param.4) | copy-start | bytes 2359300
  2.5 13.2 %collective-permute-start.4 = (bf16[4,3,32,128]{3,2,1,0:T(8,128)(2,1)S(1)}, bf16[4,3,32,128]{3,2,1,0:T(8,128)(2,1)S(1)}, u32[]{:S(2)}, u32[]{:S(2)}) collective-permute-start(bf16[4,3,32,128]{3,2,1,0:T(8,128)(2,1)S(1)} %pad_slice_fusion.4), channel_id=1, source_target_pairs={{0,8},{1,9},{2,10},{3,11}} | collective-permute-start | bytes 294920 | tf_op jit(solution)/shard_map/ppermute | solution.py:271
  3.2 12.5 %collective-permute-start.3 = (bf16[4,3,32,128]{3,2,1,0:T(8,128)(2,1)S(1)}, bf16[4,3,32,128]{3,2,1,0:T(8,128)(2,1)S(1)}, u32[]{:S(2)}, u32[]{:S(2)}) collective-permute-start(bf16[4,3,32,128]{3,2,1,0:T(8,128)(2,1)S(1)} %pad_slice_fusion.4), channel_id=1, source_target_pairs={{0,16},{1,17},{2,18},{3,19}} | collective-permute-start | bytes 294920 | tf_op jit(solution)/shard_map/ppermute | solution.py:271
  3.9 11.9 %collective-permute-start.2 = (bf16[4,3,32,128]{3,2,1,0:T(8,128)(2,1)S(1)}, bf16[4,3,32,128]{3,2,1,0:T(8,128)(2,1)S(1)}, u32[]{:S(2)}, u32[]{:S(2)}) collective-permute-start(bf16[4,3,32,128]{3,2,1,0:T(8,128)(2,1)S(1)} %pad_slice_fusion.4), channel_id=1, source_target_pairs={{4,0},{8,4},{12,8},{16,12},{20,16},{24,20},{28,24},{32,28},{36,32}... | collective-permute-start | bytes 294920 | tf_op jit(solution)/shard_map/ppermute | solution.py:268
  10.2 6.4 %collective-permute-start.1 = (bf16[7,4,32,128]{3,2,1,0:T(8,128)(2,1)S(1)}, bf16[7,4,32,128]{3,2,1,0:T(8,128)(2,1)S(1)}, u32[]{:S(2)}, u32[]{:S(2)}) collective-permute-start(bf16[7,4,32,128]{3,2,1,0:T(8,128)(2,1)S(1)} %get-tuple-element.50), channel_id=1, source_target_pairs={{1,0},{2,1},{3,2},{5,4},{6,5},{7,6},{9,8},{10,9},{11,10},{13,12},{... | collective-permute-start | bytes 688136 | tf_op jit(solution)/shard_map/ppermute | solution.py:279
  12.5 7.9 %collective-permute-start = (bf16[7,4,32,128]{3,2,1,0:T(8,128)(2,1)S(1)}, bf16[7,4,32,128]{3,2,1,0:T(8,128)(2,1)S(1)}, u32[]{:S(2)}, u32[]{:S(2)}) collective-permute-start(bf16[7,4,32,128]{3,2,1,0:T(8,128)(2,1)S(1)} %get-tuple-element.51), channel_id=1, source_target_pairs={{0,1},{1,2},{2,3},{4,5},{5,6},{6,7},{8,9},{9,10},{10,11},{12,13},{... | collective-permute-start | bytes 688136 | tf_op jit(solution)/shard_map/ppermute | solution.py:278
  16.6 3.8 %copy-start.12 = (bf16[7,4,32,128]{3,2,1,0:T(8,128)(2,1)}, bf16[7,4,32,128]{3,2,1,0:T(8,128)(2,1)S(1)}, u32[]{:S(2)}) copy-start(bf16[7,4,32,128]{3,2,1,0:T(8,128)(2,1)S(1)} %collective-permute-done.1.dn_ref) | copy-start | bytes 688132
  20.4 0.7 copy-start.13
  36.5 17.5 %collective-permute-start.11 = (bf16[38,32,128]{2,1,0:T(8,128)(2,1)S(1)}, bf16[38,32,128]{2,1,0:T(8,128)(2,1)S(1)}, u32[]{:S(2)}, u32[]{:S(2)}) collective-permute-start(bf16[38,32,128]{2,1,0:T(8,128)(2,1)S(1)} %get-tuple-element.42), channel_id=1, source_target_pairs={{28,0},{4,8},{12,16},{60,32},{36,40},{44,48},{92,64},{68,72},{76,8... | collective-permute-start | bytes 933896 | tf_op jit(solution)/shard_map/ppermute | solution.py:291
  37.8 18.1 %collective-permute-start.10 = (bf16[38,32,128]{2,1,0:T(8,128)(2,1)S(1)}, bf16[38,32,128]{2,1,0:T(8,128)(2,1)S(1)}, u32[]{:S(2)}, u32[]{:S(2)}) collective-permute-start(bf16[38,32,128]{2,1,0:T(8,128)(2,1)S(1)} %get-tuple-element.43), channel_id=1, source_target_pairs={{24,0},{0,8},{8,16},{56,32},{32,40},{40,48},{88,64},{64,72},{72,80... | collective-permute-start | bytes 933896 | tf_op jit(solution)/shard_map/ppermute | solution.py:291
  40.6 16.6 %collective-permute-start.9 = (bf16[38,32,128]{2,1,0:T(8,128)(2,1)S(1)}, bf16[38,32,128]{2,1,0:T(8,128)(2,1)S(1)}, u32[]{:S(2)}, u32[]{:S(2)}) collective-permute-start(bf16[38,32,128]{2,1,0:T(8,128)(2,1)S(1)} %get-tuple-element.44), channel_id=1, source_target_pairs={{20,0},{28,8},{4,16},{52,32},{60,40},{36,48},{84,64},{92,72},{68,8... | collective-permute-start | bytes 933896 | tf_op jit(solution)/shard_map/ppermute | solution.py:291
  41.9 15.4 %collective-permute-start.8 = (bf16[38,32,128]{2,1,0:T(8,128)(2,1)S(1)}, bf16[38,32,128]{2,1,0:T(8,128)(2,1)S(1)}, u32[]{:S(2)}, u32[]{:S(2)}) collective-permute-start(bf16[38,32,128]{2,1,0:T(8,128)(2,1)S(1)} %get-tuple-element.45), channel_id=1, source_target_pairs={{16,0},{24,8},{0,16},{48,32},{56,40},{32,48},{80,64},{88,72},{64,8... | collective-permute-start | bytes 933896 | tf_op jit(solution)/shard_map/ppermute | solution.py:291
  44.8 12.5 %collective-permute-start.7 = (bf16[38,32,128]{2,1,0:T(8,128)(2,1)S(1)}, bf16[38,32,128]{2,1,0:T(8,128)(2,1)S(1)}, u32[]{:S(2)}, u32[]{:S(2)}) collective-permute-start(bf16[38,32,128]{2,1,0:T(8,128)(2,1)S(1)} %get-tuple-element.46), channel_id=1, source_target_pairs={{12,0},{20,8},{28,16},{44,32},{52,40},{60,48},{76,64},{84,72},{92,... | collective-permute-start | bytes 933896 | tf_op jit(solution)/shard_map/ppermute | solution.py:291
  54.1 8.8 %copy-start.2 = (bf16[38,32,128]{2,1,0:T(8,128)(2,1)}, bf16[38,32,128]{2,1,0:T(8,128)(2,1)S(1)}, u32[]{:S(2)}) copy-start(bf16[38,32,128]{2,1,0:T(8,128)(2,1)S(1)} %collective-permute-done.11.refs_7_) | copy-start | bytes 933892
  54.1 8.8 %collective-permute-start.6 = (bf16[38,32,128]{2,1,0:T(8,128)(2,1)S(1)}, bf16[38,32,128]{2,1,0:T(8,128)(2,1)S(1)}, u32[]{:S(2)}, u32[]{:S(2)}) collective-permute-start(bf16[38,32,128]{2,1,0:T(8,128)(2,1)S(1)} %get-tuple-element.47), channel_id=1, source_target_pairs={{8,0},{16,8},{24,16},{40,32},{48,40},{56,48},{72,64},{80,72},{88,8... | collective-permute-start | bytes 933896 | tf_op jit(solution)/shard_map/ppermute | solution.py:291
  56.0 6.9 %copy-start.3 = (bf16[38,32,128]{2,1,0:T(8,128)(2,1)}, bf16[38,32,128]{2,1,0:T(8,128)(2,1)S(1)}, u32[]{:S(2)}) copy-start(bf16[38,32,128]{2,1,0:T(8,128)(2,1)S(1)} %collective-permute-done.10.refs_6_) | copy-start | bytes 933892
  56.0 6.9 %collective-permute-start.5 = (bf16[38,32,128]{2,1,0:T(8,128)(2,1)S(1)}, bf16[38,32,128]{2,1,0:T(8,128)(2,1)S(1)}, u32[]{:S(2)}, u32[]{:S(2)}) collective-permute-start(bf16[38,32,128]{2,1,0:T(8,128)(2,1)S(1)} %get-tuple-element.48), channel_id=1, source_target_pairs={{4,0},{12,8},{20,16},{36,32},{44,40},{52,48},{68,64},{76,72},{84,8... | collective-permute-start | bytes 933896 | tf_op jit(solution)/shard_map/ppermute | solution.py:291
  57.3 5.6 %copy-start.4 = (bf16[38,32,128]{2,1,0:T(8,128)(2,1)}, bf16[38,32,128]{2,1,0:T(8,128)(2,1)S(1)}, u32[]{:S(2)}) copy-start(bf16[38,32,128]{2,1,0:T(8,128)(2,1)S(1)} %collective-permute-done.9.refs_5_) | copy-start | bytes 933892
  57.3 5.6 %copy-start.5 = (bf16[38,32,128]{2,1,0:T(8,128)(2,1)}, bf16[38,32,128]{2,1,0:T(8,128)(2,1)S(1)}, u32[]{:S(2)}) copy-start(bf16[38,32,128]{2,1,0:T(8,128)(2,1)S(1)} %collective-permute-done.8.refs_4_) | copy-start | bytes 933892
  57.3 5.6 %copy-start.6 = (bf16[38,32,128]{2,1,0:T(8,128)(2,1)}, bf16[38,32,128]{2,1,0:T(8,128)(2,1)S(1)}, u32[]{:S(2)}) copy-start(bf16[38,32,128]{2,1,0:T(8,128)(2,1)S(1)} %collective-permute-done.7.refs_3_) | copy-start | bytes 933892
  62.9 0.7 copy-start.7
  62.9 0.8 copy-start.8
  67.9 32.2 %collective-permute-start.12 = (bf16[176,32,128]{2,1,0:T(8,128)(2,1)}, bf16[176,32,128]{2,1,0:T(8,128)(2,1)S(1)}, u32[]{:S(2)}, u32[]{:S(2)}) collective-permute-start(bf16[176,32,128]{2,1,0:T(8,128)(2,1)} %get-tuple-element.20), channel_id=1, source_target_pairs={{0,1},{1,2},{2,3},{4,5},{5,6},{6,7},{8,9},{9,10},{10,11},{12,13},{... | collective-permute-start | bytes 4325384 | tf_op jit(solution)/shard_map/ppermute | solution.py:293
  69.2 32.2 %collective-permute-start.13 = (bf16[176,32,128]{2,1,0:T(8,128)(2,1)}, bf16[176,32,128]{2,1,0:T(8,128)(2,1)}, u32[]{:S(2)}, u32[]{:S(2)}) collective-permute-start(bf16[176,32,128]{2,1,0:T(8,128)(2,1)} %get-tuple-element.21), channel_id=1, source_target_pairs={{1,0},{2,1},{3,2},{5,4},{6,5},{7,6},{9,8},{10,9},{11,10},{13,12},{... | collective-permute-start | bytes 4325384 | tf_op jit(solution)/shard_map/ppermute | solution.py:294
  100.1 2.9 copy-start.1
  146.2 14.6 %collective-permute-start.14 = (f32[16,32,128]{2,1,0:T(8,128)}, f32[16,32,128]{2,1,0:T(8,128)S(1)}, u32[]{:S(2)}, u32[]{:S(2)}) collective-permute-start(f32[16,32,128]{2,1,0:T(8,128)} %get-tuple-element.24), channel_id=1, source_target_pairs={{0,32},{1,33},{2,34},{3,35},{8,40},{9,41},{10,42},{11,43},{16,48},... | collective-permute-start | bytes 786440 | tf_op jit(solution)/shard_map/ppermute | solution.py:306
  149.6 6.0 %collective-permute-start.16 = (bf16[16,32,128]{2,1,0:T(8,128)(2,1)}, bf16[16,32,128]{2,1,0:T(8,128)(2,1)S(1)}, u32[]{:S(2)}, u32[]{:S(2)}) collective-permute-start(bf16[16,32,128]{2,1,0:T(8,128)(2,1)} %get-tuple-element.25), channel_id=1, source_target_pairs={{1,32},{2,33},{3,34},{9,40},{10,41},{11,42},{17,48},{18,49},{19,50... | collective-permute-start | bytes 393224 | tf_op jit(solution)/shard_map/ppermute | solution.py:306
  152.8 8.0 %collective-permute-start.15 = (bf16[16,32,128]{2,1,0:T(8,128)(2,1)}, bf16[16,32,128]{2,1,0:T(8,128)(2,1)S(1)}, u32[]{:S(2)}, u32[]{:S(2)}) collective-permute-start(bf16[16,32,128]{2,1,0:T(8,128)(2,1)} %get-tuple-element.25), channel_id=1, source_target_pairs={{0,33},{1,34},{2,35},{8,41},{9,42},{10,43},{16,49},{17,50},{18,51}... | collective-permute-start | bytes 393224 | tf_op jit(solution)/shard_map/ppermute | solution.py:306
  155.6 5.2 %copy-start.16 = (bf16[16,32,128]{2,1,0:T(8,128)(2,1)}, bf16[16,32,128]{2,1,0:T(8,128)(2,1)S(1)}, u32[]{:S(2)}) copy-start(bf16[16,32,128]{2,1,0:T(8,128)(2,1)S(1)} %collective-permute-done.16.below_ref) | copy-start | bytes 393220
  160.8 0.7 copy-start.18
  161.4 0.7 copy-start.10
  205.6 11.9 %collective-permute-start.17 = (f32[16,32,128]{2,1,0:T(8,128)}, f32[16,32,128]{2,1,0:T(8,128)S(1)}, u32[]{:S(2)}, u32[]{:S(2)}) collective-permute-start(f32[16,32,128]{2,1,0:T(8,128)} %get-tuple-element.26), channel_id=1, source_target_pairs={{0,32},{1,33},{2,34},{3,35},{8,40},{9,41},{10,42},{11,43},{16,48},... | collective-permute-start | bytes 786440 | tf_op jit(solution)/shard_map/ppermute | solution.py:306
  207.6 5.6 %collective-permute-start.19 = (bf16[16,32,128]{2,1,0:T(8,128)(2,1)}, bf16[16,32,128]{2,1,0:T(8,128)(2,1)S(1)}, u32[]{:S(2)}, u32[]{:S(2)}) collective-permute-start(bf16[16,32,128]{2,1,0:T(8,128)(2,1)} %get-tuple-element.27), channel_id=1, source_target_pairs={{1,32},{2,33},{3,34},{9,40},{10,41},{11,42},{17,48},{18,49},{19,50... | collective-permute-start | bytes 393224 | tf_op jit(solution)/shard_map/ppermute | solution.py:306
  208.9 8.6 %collective-permute-start.18 = (bf16[16,32,128]{2,1,0:T(8,128)(2,1)}, bf16[16,32,128]{2,1,0:T(8,128)(2,1)S(1)}, u32[]{:S(2)}, u32[]{:S(2)}) collective-permute-start(bf16[16,32,128]{2,1,0:T(8,128)(2,1)} %get-tuple-element.27), channel_id=1, source_target_pairs={{0,33},{1,34},{2,35},{8,41},{9,42},{10,43},{16,49},{17,50},{18,51}... | collective-permute-start | bytes 393224 | tf_op jit(solution)/shard_map/ppermute | solution.py:306
  213.2 4.3 %copy-start.17 = (bf16[16,32,128]{2,1,0:T(8,128)(2,1)}, bf16[16,32,128]{2,1,0:T(8,128)(2,1)S(1)}, u32[]{:S(2)}) copy-start(bf16[16,32,128]{2,1,0:T(8,128)(2,1)S(1)} %collective-permute-done.19.below_ref) | copy-start | bytes 393220
  218.2 0.7 copy-start.11
  262.2 11.8 %collective-permute-start.20 = (f32[16,32,128]{2,1,0:T(8,128)}, f32[16,32,128]{2,1,0:T(8,128)S(1)}, u32[]{:S(2)}, u32[]{:S(2)}) collective-permute-start(f32[16,32,128]{2,1,0:T(8,128)} %get-tuple-element.28), channel_id=1, source_target_pairs={{0,32},{1,33},{2,34},{3,35},{8,40},{9,41},{10,42},{11,43},{16,48},... | collective-permute-start | bytes 786440 | tf_op jit(solution)/shard_map/ppermute | solution.py:306
  264.1 5.6 %collective-permute-start.22 = (bf16[16,32,128]{2,1,0:T(8,128)(2,1)}, bf16[16,32,128]{2,1,0:T(8,128)(2,1)S(1)}, u32[]{:S(2)}, u32[]{:S(2)}) collective-permute-start(bf16[16,32,128]{2,1,0:T(8,128)(2,1)} %get-tuple-element.29), channel_id=1, source_target_pairs={{1,32},{2,33},{3,34},{9,40},{10,41},{11,42},{17,48},{18,49},{19,50... | collective-permute-start | bytes 393224 | tf_op jit(solution)/shard_map/ppermute | solution.py:306
  265.4 8.6 %collective-permute-start.21 = (bf16[16,32,128]{2,1,0:T(8,128)(2,1)}, bf16[16,32,128]{2,1,0:T(8,128)(2,1)S(1)}, u32[]{:S(2)}, u32[]{:S(2)}) collective-permute-start(bf16[16,32,128]{2,1,0:T(8,128)(2,1)} %get-tuple-element.29), channel_id=1, source_target_pairs={{0,33},{1,34},{2,35},{8,41},{9,42},{10,43},{16,49},{17,50},{18,51}... | collective-permute-start | bytes 393224 | tf_op jit(solution)/shard_map/ppermute | solution.py:306
  269.7 4.3 %copy-start.14 = (bf16[16,32,128]{2,1,0:T(8,128)(2,1)}, bf16[16,32,128]{2,1,0:T(8,128)(2,1)S(1)}, u32[]{:S(2)}) copy-start(bf16[16,32,128]{2,1,0:T(8,128)(2,1)S(1)} %collective-permute-done.22.below_ref) | copy-start | bytes 393220
  274.7 0.7 copy-start.9
  321.5 11.2 %collective-permute-start.23 = (bf16[2,16,32,128]{3,2,1,0:T(8,128)(2,1)}, bf16[2,16,32,128]{3,2,1,0:T(8,128)(2,1)}, u32[]{:S(2)}, u32[]{:S(2)}) collective-permute-start(bf16[2,16,32,128]{3,2,1,0:T(8,128)(2,1)} %get-tuple-element.40), channel_id=1, source_target_pairs={{0,4},{8,12},{16,20},{32,36},{40,44},{48,52},{64,68},{72,76},{80,8... | collective-permute-start | bytes 786440 | tf_op jit(solution)/shard_map/ppermute | solution.py:319
  323.5 11.5 %collective-permute-start.24 = (bf16[2,16,32,128]{3,2,1,0:T(8,128)(2,1)}, bf16[2,16,32,128]{3,2,1,0:T(8,128)(2,1)}, u32[]{:S(2)}, u32[]{:S(2)}) collective-permute-start(bf16[2,16,32,128]{3,2,1,0:T(8,128)(2,1)} %get-tuple-element.39), channel_id=1, source_target_pairs={{0,8},{8,16},{16,24},{32,40},{40,48},{48,56},{64,72},{72,80},{80,8... | collective-permute-start | bytes 786440 | tf_op jit(solution)/shard_map/ppermute | solution.py:319
  328.1 17.0 %collective-permute-start.29 = (bf16[2,16,32,128]{3,2,1,0:T(8,128)(2,1)S(1)}, bf16[2,16,32,128]{3,2,1,0:T(8,128)(2,1)S(1)}, u32[]{:S(2)}, u32[]{:S(2)}) collective-permute-start(bf16[2,16,32,128]{3,2,1,0:T(8,128)(2,1)S(1)} %get-tuple-element.34), channel_id=1, source_target_pairs={{0,28},{8,4},{16,12},{32,60},{40,36},{48,44},{64,92},{72,68},{80,7... | collective-permute-start | bytes 786440 | tf_op jit(solution)/shard_map/ppermute | solution.py:319
  329.4 15.6 %collective-permute-start.28 = (bf16[2,16,32,128]{3,2,1,0:T(8,128)(2,1)}, bf16[2,16,32,128]{3,2,1,0:T(8,128)(2,1)S(1)}, u32[]{:S(2)}, u32[]{:S(2)}) collective-permute-start(bf16[2,16,32,128]{3,2,1,0:T(8,128)(2,1)} %get-tuple-element.35), channel_id=1, source_target_pairs={{0,24},{8,0},{16,8},{32,56},{40,32},{48,40},{64,88},{72,64},{80,72... | collective-permute-start | bytes 786440 | tf_op jit(solution)/shard_map/ppermute | solution.py:319
  331.4 13.7 %collective-permute-start.27 = (bf16[2,16,32,128]{3,2,1,0:T(8,128)(2,1)}, bf16[2,16,32,128]{3,2,1,0:T(8,128)(2,1)S(1)}, u32[]{:S(2)}, u32[]{:S(2)}) collective-permute-start(bf16[2,16,32,128]{3,2,1,0:T(8,128)(2,1)} %get-tuple-element.36), channel_id=1, source_target_pairs={{0,20},{8,28},{16,4},{32,52},{40,60},{48,36},{64,84},{72,92},{80,6... | collective-permute-start | bytes 786440 | tf_op jit(solution)/shard_map/ppermute | solution.py:319
  332.7 7.0 %collective-permute-start.25 = (bf16[2,16,32,128]{3,2,1,0:T(8,128)(2,1)}, bf16[2,16,32,128]{3,2,1,0:T(8,128)(2,1)S(1)}, u32[]{:S(2)}, u32[]{:S(2)}) collective-permute-start(bf16[2,16,32,128]{3,2,1,0:T(8,128)(2,1)} %get-tuple-element.38), channel_id=1, source_target_pairs={{0,12},{8,20},{16,28},{32,44},{40,52},{48,60},{64,76},{72,84},{80,... | collective-permute-start | bytes 786440 | tf_op jit(solution)/shard_map/ppermute | solution.py:319
  335.0 10.0 %collective-permute-start.26 = (bf16[2,16,32,128]{3,2,1,0:T(8,128)(2,1)}, bf16[2,16,32,128]{3,2,1,0:T(8,128)(2,1)S(1)}, u32[]{:S(2)}, u32[]{:S(2)}) collective-permute-start(bf16[2,16,32,128]{3,2,1,0:T(8,128)(2,1)} %get-tuple-element.37), channel_id=1, source_target_pairs={{0,16},{8,24},{16,0},{32,48},{40,56},{48,32},{64,80},{72,88},{80,6... | collective-permute-start | bytes 786440 | tf_op jit(solution)/shard_map/ppermute | solution.py:319
  (2 other events, 1.3 us)

commit v2 on v1

--- a/solution.py
+++ b/solution.py
@@ -179,28 +179,29 @@
 
     for q, rows in enumerate(PHASE):
 
-        def step(i, carry, q=q, rows=rows):
-            s = 4 * q + i
-            now, later = lax.rem(s, 2), lax.rem(s + 1, 2)
-            matrix = banded(w_ref[s])
-            res_ref[lax.rem(s // 2 - sub + SUB, SUB), lax.rem(s, 2)] = xs[now, 1, BAND + 1 : 2 * BAND + 1]
-            for row in range(BAND - rows, 2 * BAND + rows, 4):
-                for k, t in enumerate(block(xs, now, matrix, row)):
-                    r = row + 2 * k
-                    if r < BAND:
-                        at = OFFSET[q] + i * rows + (r - (BAND - rows))
-                        d = up_ref[pl.ds(at, 2)]
-                    elif r < 2 * BAND:
-                        d = d_ref[s, r - BAND : r - BAND + 2]
-                    else:
-                        at = OFFSET[q] + i * rows + (r - 2 * BAND)
-                        d = dn_ref[pl.ds(at, 2)]
-                    x = state[r : r + 2].reshape(2 * C, W) + (M * H) * t + d.astype(f32).reshape(2 * C, W)
-                    state[r : r + 2] = x.reshape(2, C, W)
-                    put(later, r, x)
+        def two_steps(half, carry, q=q, rows=rows):
+            for now in range(2):
+                i = 2 * half + now
+                s = 4 * q + i
+                matrix = banded(w_ref[s])
+                res_ref[lax.rem(2 * q + half - sub + SUB, SUB), now] = xs[now, 1, BAND + 1 : 2 * BAND + 1]
+                for row in range(BAND - rows, 2 * BAND + rows, 4):
+                    for k, t in enumerate(block(xs, now, matrix, row)):
+                        r = row + 2 * k
+                        if r < BAND:
+                            at = OFFSET[q] + i * rows + (r - (BAND - rows))
+                            d = up_ref[pl.ds(at, 2)]
+                        elif r < 2 * BAND:
+                            d = d_ref[s, r - BAND : r - BAND + 2]
+                        else:
+                            at = OFFSET[q] + i * rows + (r - 2 * BAND)
+                            d = dn_ref[pl.ds(at, 2)]
+                        x = state[r : r + 2].reshape(2 * C, W) + (M * H) * t + d.astype(f32).reshape(2 * C, W)
+                        state[r : r + 2] = x.reshape(2, C, W)
+                        put(1 - now, r, x)
             return carry
 
-        lax.fori_loop(0, 4, step, 0)
+        lax.fori_loop(0, 2, two_steps, 0)
     out_ref[...] = state[BAND : 2 * BAND]
     edge_ref[...] = state[BAND : 2 * BAND].astype(bf16)
 
@@ -290,26 +291,26 @@
         ]
         received.append(lax.ppermute(value, "layer", pairs))
     d, w, up, dn = pack(sub.astype(jnp.int32).reshape(1), received, v1)
-    above = lax.ppermute(up, "rows", [(i, i + 1) for i in range(rows - 1)])
-    below = lax.ppermute(dn, "rows", [(i + 1, i) for i in range(rows - 1)])
-
-    info = jnp.stack([z, sub, jnp.where(group == 0, 1, 0)]).astype(jnp.int32)
-    def handoff(value, by):
+
+    def among_sweepers(value, ahead, by):
         pairs = []
-        for g in range(groups - 1):
+        for g in range(groups - ahead):
             for b in range(IMAGES):
                 for k in range(rows):
                     if 0 <= k + by < rows:
                         source = (SUB * g + home(b)) * rows + k
-                        target = (SUB * (g + 1) + home(b)) * rows + k + by
+                        target = (SUB * (g + ahead) + home(b)) * rows + k + by
                         pairs.append((source, target))
         return lax.ppermute(value, ("layer", "rows"), pairs)
 
+    above, below = among_sweepers(up, 0, 1), among_sweepers(dn, 0, -1)
+
+    info = jnp.stack([z, sub, jnp.where(group == 0, 1, 0)]).astype(jnp.int32)
     state, low, high = v1, above[HALO:], below[HALO:]
     for stage in range(groups):
         results, state, edge = sweep(info, v1, state, low, high, d, above, below, w)
         if stage < groups - 1:
-            state, low, high = handoff(state, 0), handoff(edge, 1), handoff(edge, -1)
+            state, low, high = among_sweepers(state, 1, 0), among_sweepers(edge, 1, 1), among_sweepers(edge, 1, -1)
 
     slots = [results[0]]
     for r in range(1, SUB):

time: 351 us -> 217 us (0.62)
  Pallas kernels: 190 us -> 69.1 us
  waiting for transfers between devices: 69.9 us -> 59.1 us
    pallas_call x4, Pallas kernels: 173 us -> 52.6 us  [sweep(): pl.pallas_call(sweep_kernel, out_shape=(shape(SUB, 2, BAND, C, W), shape(...]
    ppermute x11, waiting for transfers between devices: 46.4 us -> 35.6 us  [among_sweepers(): return lax.ppermute(value, ('layer', 'rows'), pairs)]
  transfers between devices with their start and end apart: 30 -> 30, of which waited for: 14 -> 14; matrix products, arithmetic and copies ran while one was open for 2% -> 4% of each run, Pallas kernels for 0% -> 0%
where the time goes in v2:
time: 217 us; the launch traced here: 213 us
  Pallas kernels  69.1 us (32%)
  waiting for transfers between devices  59.1 us (27%)
  starting transfers between devices  58.7 us (27%)
  local copies, waits for them, and re-layouts  21.6 us (10%)
  other arithmetic  4.19 us (2%)
    pallas_call x4, Pallas kernels, sweep(): pl.pallas_call(sweep_kernel, out_shape=(shape(SUB, 2, BAND, C, W), shape(...  52.6 us
    ppermute x11, waiting for transfers between devices, among_sweepers(): return lax.ppermute(value, ('layer', 'rows'), pairs)  35.6 us
    ppermute x11, starting transfers between devices, among_sweepers(): return lax.ppermute(value, ('layer', 'rows'), pairs)  24 us
    ppermute x7, waiting for transfers between devices, per_device(): received.append(lax.ppermute(value, 'layer', pairs))  14.1 us
    ppermute x7, starting transfers between devices, per_device(): slots.append(lax.ppermute(results[r], 'layer', pairs))  13.3 us
    pallas_call x1, Pallas kernels, relax(): pl.pallas_call(relax_kernel, out_shape=(shape(IMAGES, CHUNK, C, W), shape...  12.4 us
    ppermute x7, starting transfers between devices, per_device(): received.append(lax.ppermute(value, 'layer', pairs))  12.1 us
    unnamed x46, local copies, waits for them, and re-layouts  7.71 us
  transfers between devices with their start and end apart: 30, of which 14 were waited for; matrix products, arithmetic and copies ran while one was open for 4% of the time, Pallas kernels for 0%

profile of v2, /device:TPU:100, one launch (start us, length us, event | category | flops | bytes accessed | tf_op | source)
XLA Modules:
  0.0 213.4 jit_solution(12624075561908914431)
XLA Ops:
  0.0 1.7 reshape.13
  3.9 4.3 %collective-permute-start.2 = (bf16[4,3,32,128]{3,2,1,0:T(8,128)(2,1)S(1)}, bf16[4,3,32,128]{3,2,1,0:T(8,128)(2,1)S(1)}, u32[]{:S(2)}, u32[]{:S(2)}) collective-permute-start(bf16[4,3,32,128]{3,2,1,0:T(8,128)(2,1)S(1)} %pad_slice_fusion.4), channel_id=1, source_target_pairs={{4,0},{8,4},{12,8},{16,12},{20,16},{24,20},{28,24},{32,28},{36,32}... | collective-permute-start | bytes 294920 | tf_op jit(solution)/shard_map/ppermute | solution.py:269
  8.4 1.5 convert_element_type.20
  10.2 2.3 %collective-permute-start.1 = (bf16[7,4,32,128]{3,2,1,0:T(8,128)(2,1)S(1)}, bf16[7,4,32,128]{3,2,1,0:T(8,128)(2,1)S(1)}, u32[]{:S(2)}, u32[]{:S(2)}) collective-permute-start(bf16[7,4,32,128]{3,2,1,0:T(8,128)(2,1)S(1)} %get-tuple-element.50), channel_id=1, source_target_pairs={{1,0},{2,1},{3,2},{5,4},{6,5},{7,6},{9,8},{10,9},{11,10},{13,12},{... | collective-permute-start | bytes 688136 | tf_op jit(solution)/shard_map/ppermute | solution.py:280
  12.5 1.3 collective-permute-start
  16.6 3.8 %collective-permute-done.up_ref = bf16[7,4,32,128]{3,2,1,0:T(8,128)(2,1)S(1)} collective-permute-done((bf16[7,4,32,128]{3,2,1,0:T(8,128)(2,1)S(1)}, bf16[7,4,32,128]{3,2,1,0:T(8,128)(2,1)S(1)}, u32[]{:S(2)}, u32[]{:S(2)}) %collective-permute-start) | collective-permute-done | bytes 229408 | tf_op jit(solution)/shard_map/ppermute | solution.py:279
  21.1 12.4 %relax.1 = (bf16[3,38,32,128]{3,2,1,0:T(8,128)(2,1)}, f32[16,32,128]{2,1,0:T(8,128)}) custom-call(s32[1]{0:T(128)} %bitcast.z_ref, bf16[7,16,32,128]{3,2,1,0:T(8,128)(2,1)} %pad_maximum_fusion.own_ref, bf16[7,4,32,128]{3,2,1,0:T(8,128)(2,1)} %copy-done.13, bf16[7,4,32,128]{3,2,1,0:T(8,128)(2,1)} %copy-done.12, f32[16,32,128]{2,1,0:T(8,128)} %bitcast.75, ...), custom_call_target="tpu_custom_call" | custom-call | tf_op jit(solution)/shard_map/relax/pallas_call | solution.py:218
  33.5 3.0 %dynamic-slice_bitcast_fusion = (bf16[38,32,128]{2,1,0:T(8,128)(2,1)S(1)}, bf16[38,32,128]{2,1,0:T(8,128)(2,1)S(1)}, bf16[38,32,128]{2,1,0:T(8,128)(2,1)S(1)}, b...) fusion(bf16[3,38,32,128]{3,2,1,0:T(8,128)(2,1)} %get-tuple-elem, ...), kind=kLoop, calls=%fused_computation.6 | loop fusion | bytes 4980768 | tf_op jit(solution)/shard_map/jit(dynamic_index_in_dim)/squeeze | solution.py:288
  37.8 2.8 %collective-permute-start.10 = (bf16[38,32,128]{2,1,0:T(8,128)(2,1)S(1)}, bf16[38,32,128]{2,1,0:T(8,128)(2,1)S(1)}, u32[]{:S(2)}, u32[]{:S(2)}) collective-permute-start(bf16[38,32,128]{2,1,0:T(8,128)(2,1)S(1)} %get-tuple-element.43), channel_id=1, source_target_pairs={{24,0},{0,8},{8,16},{56,32},{32,40},{40,48},{88,64},{64,72},{72,80... | collective-permute-start | bytes 933896 | tf_op jit(solution)/shard_map/ppermute | solution.py:292
  40.6 1.3 collective-permute-start.9
  41.9 2.9 %collective-permute-start.8 = (bf16[38,32,128]{2,1,0:T(8,128)(2,1)S(1)}, bf16[38,32,128]{2,1,0:T(8,128)(2,1)S(1)}, u32[]{:S(2)}, u32[]{:S(2)}) collective-permute-start(bf16[38,32,128]{2,1,0:T(8,128)(2,1)S(1)} %get-tuple-element.45), channel_id=1, source_target_pairs={{16,0},{24,8},{0,16},{48,32},{56,40},{32,48},{80,64},{88,72},{64,8... | collective-permute-start | bytes 933896 | tf_op jit(solution)/shard_map/ppermute | solution.py:292
  44.8 1.3 collective-permute-start.7
  46.1 7.9 %collective-permute-done.11.refs_7_ = bf16[38,32,128]{2,1,0:T(8,128)(2,1)S(1)} collective-permute-done((bf16[38,32,128]{2,1,0:T(8,128)(2,1)S(1)}, bf16[38,32,128]{2,1,0:T(8,128)(2,1)S(1)}, u32[]{:S(2)}, u32[]{:S(2)}) %collective-permute-start.11) | collective-permute-done | bytes 311328 | tf_op jit(solution)/shard_map/ppermute | solution.py:292
  54.1 1.3 collective-permute-start.6
  57.3 5.6 %collective-permute-done.6.refs_2_ = bf16[38,32,128]{2,1,0:T(8,128)(2,1)S(1)} collective-permute-done((bf16[38,32,128]{2,1,0:T(8,128)(2,1)S(1)}, bf16[38,32,128]{2,1,0:T(8,128)(2,1)S(1)}, u32[]{:S(2)}, u32[]{:S(2)}) %collective-permute-start.6) | collective-permute-done | bytes 311328 | tf_op jit(solution)/shard_map/ppermute | solution.py:292
  63.7 4.1 %pack.1 = (bf16[16,16,32,128]{3,2,1,0:T(8,128)(2,1)}, bf16[16,3,32,128]{3,2,1,0:T(8,128)(2,1)}, bf16[176,32,128]{2,1,0:T(8,128)(2,1)}, bf16[176,32,128]{2,1,0:T(8,128)(2,1)}) custom-call(s32[1]{0:T(128)} %bitcast.1.sub_ref, bf16[38,32,128]{2,1,0:T(8,128)(2,1)} %get-tuple-element.49.refs_0_, bf16[38,32,128]{2,1,0:T(8,128)(2,1)} %copy-done.8, ...), custom_call_target="tpu_custom_call" | custom-call | tf_op jit(solution)/shard_map/pack/pallas_call | solution.py:233
  69.2 5.7 %collective-permute-start.13 = (bf16[176,32,128]{2,1,0:T(8,128)(2,1)}, bf16[176,32,128]{2,1,0:T(8,128)(2,1)}, u32[]{:S(2)}, u32[]{:S(2)}) collective-permute-start(bf16[176,32,128]{2,1,0:T(8,128)(2,1)} %get-tuple-element.21), channel_id=1, source_target_pairs={{1,0},{2,1},{3,2},{9,8},{10,9},{11,10},{17,16},{18,17},{19,18},{33... | collective-permute-start | bytes 4325384 | tf_op jit(solution)/shard_map/ppermute | solution.py:304
  75.5 13.4 %collective-permute-done.12.up_ref = bf16[176,32,128]{2,1,0:T(8,128)(2,1)S(1)} collective-permute-done((bf16[176,32,128]{2,1,0:T(8,128)(2,1)}, bf16[176,32,128]{2,1,0:T(8,128)(2,1)S(1)}, u32[]{:S(2)}, u32[]{:S(2)}) %collective-permute-start.12) | collective-permute-done | bytes 1441824 | tf_op jit(solution)/shard_map/ppermute | solution.py:304
  90.5 1.6 slice.64.below_ref
  92.1 13.0 %sweep.4 = (bf16[8,2,16,32,128]{4,3,2,1,0:T(8,128)(2,1)}, f32[16,32,128]{2,1,0:T(8,128)}, bf16[16,32,128]{2,1,0:T(8,128)(2,1)}) custom-call(s32[3]{0:T(128)} %pad_add_fusion.info_ref, f32[16,32,128]{2,1,0:T(8,128)} %get-tuple-element.18.refs_8_.v1_ref.own_ref, f32[16,32,128]{2,1,0:T(8,128)} %get-tuple-element.18.refs_8_.v1_ref.own_ref, ...), custom_call_target="tpu_custom_call" | custom-call | tf_op jit(solution)/shard_map/sweep/pallas_call | solution.py:248
  105.2 3.4 %collective-permute-start.14 = (f32[16,32,128]{2,1,0:T(8,128)}, f32[16,32,128]{2,1,0:T(8,128)S(1)}, u32[]{:S(2)}, u32[]{:S(2)}) collective-permute-start(f32[16,32,128]{2,1,0:T(8,128)} %get-tuple-element.24), channel_id=1, source_target_pairs={{0,32},{1,33},{2,34},{3,35},{8,40},{9,41},{10,42},{11,43},{16,48},... | collective-permute-start | bytes 786440 | tf_op jit(solution)/shard_map/ppermute | solution.py:304
  108.6 3.2 %collective-permute-start.16 = (bf16[16,32,128]{2,1,0:T(8,128)(2,1)}, bf16[16,32,128]{2,1,0:T(8,128)(2,1)S(1)}, u32[]{:S(2)}, u32[]{:S(2)}) collective-permute-start(bf16[16,32,128]{2,1,0:T(8,128)(2,1)} %get-tuple-element.25), channel_id=1, source_target_pairs={{1,32},{2,33},{3,34},{9,40},{10,41},{11,42},{17,48},{18,49},{19,50... | collective-permute-start | bytes 393224 | tf_op jit(solution)/shard_map/ppermute | solution.py:304
  111.8 1.3 collective-permute-start.15
  113.1 1.5 collective-permute-done.16.below_ref
  114.6 5.2 %collective-permute-done.15.above_ref = bf16[16,32,128]{2,1,0:T(8,128)(2,1)S(1)} collective-permute-done((bf16[16,32,128]{2,1,0:T(8,128)(2,1)}, bf16[16,32,128]{2,1,0:T(8,128)(2,1)S(1)}, u32[]{:S(2)}, u32[]{:S(2)}) %collective-permute-start.15) | collective-permute-done | bytes 131104 | tf_op jit(solution)/shard_map/ppermute | solution.py:304
  121.1 13.2 %sweep.5 = (bf16[8,2,16,32,128]{4,3,2,1,0:T(8,128)(2,1)}, f32[16,32,128]{2,1,0:T(8,128)}, bf16[16,32,128]{2,1,0:T(8,128)(2,1)}) custom-call(s32[3]{0:T(128)} %pad_add_fusion.info_ref, f32[16,32,128]{2,1,0:T(8,128)} %get-tuple-element.18.refs_8_.v1_ref.own_ref, f32[16,32,128]{2,1,0:T(8,128)} %copy-done.10, bf16[16,32,128]{2,1,0:T(8,128)(2,1)} %copy-done.18, ...), custom_call_target="tpu_custom_call" | custom-call | tf_op jit(solution)/shard_map/sweep/pallas_call | solution.py:248
  134.4 2.0 collective-permute-start.17
  136.4 1.3 collective-permute-start.19
  137.7 1.3 collective-permute-start.18
  139.0 3.0 %collective-permute-done.19.below_ref = bf16[16,32,128]{2,1,0:T(8,128)(2,1)S(1)} collective-permute-done((bf16[16,32,128]{2,1,0:T(8,128)(2,1)}, bf16[16,32,128]{2,1,0:T(8,128)(2,1)S(1)}, u32[]{:S(2)}, u32[]{:S(2)}) %collective-permute-start.19) | collective-permute-done | bytes 131104 | tf_op jit(solution)/shard_map/ppermute | solution.py:304
  141.9 4.3 %collective-permute-done.18.above_ref = bf16[16,32,128]{2,1,0:T(8,128)(2,1)S(1)} collective-permute-done((bf16[16,32,128]{2,1,0:T(8,128)(2,1)}, bf16[16,32,128]{2,1,0:T(8,128)(2,1)S(1)}, u32[]{:S(2)}, u32[]{:S(2)}) %collective-permute-start.18) | collective-permute-done | bytes 131104 | tf_op jit(solution)/shard_map/ppermute | solution.py:304
  147.6 13.1 %sweep.6 = (bf16[8,2,16,32,128]{4,3,2,1,0:T(8,128)(2,1)}, f32[16,32,128]{2,1,0:T(8,128)}, bf16[16,32,128]{2,1,0:T(8,128)(2,1)}) custom-call(s32[3]{0:T(128)} %pad_add_fusion.info_ref, f32[16,32,128]{2,1,0:T(8,128)} %get-tuple-element.18.refs_8_.v1_ref.own_ref, f32[16,32,128]{2,1,0:T(8,128)} %copy-done.11, bf16[16,32,128]{2,1,0:T(8,128)(2,1)} %copy-done.19, ...), custom_call_target="tpu_custom_call" | custom-call | tf_op jit(solution)/shard_map/sweep/pallas_call | solution.py:248
  160.7 1.9 collective-permute-start.20
  162.6 1.3 collective-permute-start.22
  163.9 1.3 collective-permute-start.21
  165.2 3.0 %collective-permute-done.22.below_ref = bf16[16,32,128]{2,1,0:T(8,128)(2,1)S(1)} collective-permute-done((bf16[16,32,128]{2,1,0:T(8,128)(2,1)}, bf16[16,32,128]{2,1,0:T(8,128)(2,1)S(1)}, u32[]{:S(2)}, u32[]{:S(2)}) %collective-permute-start.22) | collective-permute-done | bytes 131104 | tf_op jit(solution)/shard_map/ppermute | solution.py:304
  168.2 4.3 %collective-permute-done.21.above_ref = bf16[16,32,128]{2,1,0:T(8,128)(2,1)S(1)} collective-permute-done((bf16[16,32,128]{2,1,0:T(8,128)(2,1)}, bf16[16,32,128]{2,1,0:T(8,128)(2,1)S(1)}, u32[]{:S(2)}, u32[]{:S(2)}) %collective-permute-start.21) | collective-permute-done | bytes 131104 | tf_op jit(solution)/shard_map/ppermute | solution.py:304
  173.9 13.2 %sweep.7 = (bf16[8,2,16,32,128]{4,3,2,1,0:T(8,128)(2,1)}, f32[16,32,128]{2,1,0:T(8,128)}, bf16[16,32,128]{2,1,0:T(8,128)(2,1)}) custom-call(s32[3]{0:T(128)} %pad_add_fusion.info_ref, f32[16,32,128]{2,1,0:T(8,128)} %get-tuple-element.18.refs_8_.v1_ref.own_ref, f32[16,32,128]{2,1,0:T(8,128)} %copy-done.9, bf16[16,32,128]{2,1,0:T(8,128)(2,1)} %copy-done.15, ...), custom_call_target="tpu_custom_call" | custom-call | tf_op jit(solution)/shard_map/sweep/pallas_call | solution.py:248
  187.1 2.9 %slice_bitcast_fusion = (bf16[2,16,32,128]{3,2,1,0:T(8,128)(2,1)S(1)}, bf16[2,16,32,128]{3,2,1,0:T(8,128)(2,1)}, bf16[2,16,32,128]{3,2,1,0:T(8,128)(2,1)}, bf16[...) fusion(bf16[8,2,16,32,128]{4,3,2,1,0:T(8,128)(2,1)} %get-tuple-, ...), kind=kLoop, calls=%fused_computation.26 | loop fusion | bytes 4194304 | tf_op jit(solution)/shard_map/squeeze | solution.py:320
  190.0 2.0 collective-permute-start.23
  192.0 2.1 %collective-permute-start.24 = (bf16[2,16,32,128]{3,2,1,0:T(8,128)(2,1)}, bf16[2,16,32,128]{3,2,1,0:T(8,128)(2,1)}, u32[]{:S(2)}, u32[]{:S(2)}) collective-permute-start(bf16[2,16,32,128]{3,2,1,0:T(8,128)(2,1)} %get-tuple-element.39), channel_id=1, source_target_pairs={{0,8},{8,16},{16,24},{32,40},{40,48},{48,56},{64,72},{72,80},{80,8... | collective-permute-start | bytes 786440 | tf_op jit(solution)/shard_map/ppermute | solution.py:320
  194.1 1.3 collective-permute-start.29
  195.4 1.9 collective-permute-start.28
  197.3 1.3 collective-permute-start.27
  198.7 1.3 collective-permute-start.25
  201.0 3.3 %collective-permute-start.26 = (bf16[2,16,32,128]{3,2,1,0:T(8,128)(2,1)}, bf16[2,16,32,128]{3,2,1,0:T(8,128)(2,1)S(1)}, u32[]{:S(2)}, u32[]{:S(2)}) collective-permute-start(bf16[2,16,32,128]{3,2,1,0:T(8,128)(2,1)} %get-tuple-element.37), channel_id=1, source_target_pairs={{0,16},{8,24},{16,0},{32,48},{40,56},{48,32},{64,80},{72,88},{80,6... | collective-permute-start | bytes 786440 | tf_op jit(solution)/shard_map/ppermute | solution.py:320
  205.7 5.3 %collective-permute-done.26 = bf16[2,16,32,128]{3,2,1,0:T(8,128)(2,1)S(1)} collective-permute-done((bf16[2,16,32,128]{3,2,1,0:T(8,128)(2,1)}, bf16[2,16,32,128]{3,2,1,0:T(8,128)(2,1)S(1)}, u32[]{:S(2)}, u32[]{:S(2)}) %collective-permute-start.26) | collective-permute-done | bytes 262176 | tf_op jit(solution)/shard_map/ppermute | solution.py:320
  211.4 2.0 copy.10
  (86 shorter events, 20.0 us)
Async XLA Ops:
  0.0 8.3 %copy-start = (f32[3,32,16,128]{3,2,1,0:T(8,128)S(1)}, f32[3,32,16,128]{3,2,1,0:T(8,128)}, u32[]{:S(2)}) copy-start(f32[3,32,16,128]{3,2,1,0:T(8,128)} %param.4) | copy-start | bytes 2359300
  2.5 13.2 %collective-permute-start.4 = (bf16[4,3,32,128]{3,2,1,0:T(8,128)(2,1)S(1)}, bf16[4,3,32,128]{3,2,1,0:T(8,128)(2,1)S(1)}, u32[]{:S(2)}, u32[]{:S(2)}) collective-permute-start(bf16[4,3,32,128]{3,2,1,0:T(8,128)(2,1)S(1)} %pad_slice_fusion.4), channel_id=1, source_target_pairs={{0,8},{1,9},{2,10},{3,11}} | collective-permute-start | bytes 294920 | tf_op jit(solution)/shard_map/ppermute | solution.py:272
  3.2 12.5 %collective-permute-start.3 = (bf16[4,3,32,128]{3,2,1,0:T(8,128)(2,1)S(1)}, bf16[4,3,32,128]{3,2,1,0:T(8,128)(2,1)S(1)}, u32[]{:S(2)}, u32[]{:S(2)}) collective-permute-start(bf16[4,3,32,128]{3,2,1,0:T(8,128)(2,1)S(1)} %pad_slice_fusion.4), channel_id=1, source_target_pairs={{0,16},{1,17},{2,18},{3,19}} | collective-permute-start | bytes 294920 | tf_op jit(solution)/shard_map/ppermute | solution.py:272
  3.9 11.9 %collective-permute-start.2 = (bf16[4,3,32,128]{3,2,1,0:T(8,128)(2,1)S(1)}, bf16[4,3,32,128]{3,2,1,0:T(8,128)(2,1)S(1)}, u32[]{:S(2)}, u32[]{:S(2)}) collective-permute-start(bf16[4,3,32,128]{3,2,1,0:T(8,128)(2,1)S(1)} %pad_slice_fusion.4), channel_id=1, source_target_pairs={{4,0},{8,4},{12,8},{16,12},{20,16},{24,20},{28,24},{32,28},{36,32}... | collective-permute-start | bytes 294920 | tf_op jit(solution)/shard_map/ppermute | solution.py:269
  10.2 6.4 %collective-permute-start.1 = (bf16[7,4,32,128]{3,2,1,0:T(8,128)(2,1)S(1)}, bf16[7,4,32,128]{3,2,1,0:T(8,128)(2,1)S(1)}, u32[]{:S(2)}, u32[]{:S(2)}) collective-permute-start(bf16[7,4,32,128]{3,2,1,0:T(8,128)(2,1)S(1)} %get-tuple-element.50), channel_id=1, source_target_pairs={{1,0},{2,1},{3,2},{5,4},{6,5},{7,6},{9,8},{10,9},{11,10},{13,12},{... | collective-permute-start | bytes 688136 | tf_op jit(solution)/shard_map/ppermute | solution.py:280
  12.5 7.9 %collective-permute-start = (bf16[7,4,32,128]{3,2,1,0:T(8,128)(2,1)S(1)}, bf16[7,4,32,128]{3,2,1,0:T(8,128)(2,1)S(1)}, u32[]{:S(2)}, u32[]{:S(2)}) collective-permute-start(bf16[7,4,32,128]{3,2,1,0:T(8,128)(2,1)S(1)} %get-tuple-element.51), channel_id=1, source_target_pairs={{0,1},{1,2},{2,3},{4,5},{5,6},{6,7},{8,9},{9,10},{10,11},{12,13},{... | collective-permute-start | bytes 688136 | tf_op jit(solution)/shard_map/ppermute | solution.py:279
  16.6 3.8 %copy-start.12 = (bf16[7,4,32,128]{3,2,1,0:T(8,128)(2,1)}, bf16[7,4,32,128]{3,2,1,0:T(8,128)(2,1)S(1)}, u32[]{:S(2)}) copy-start(bf16[7,4,32,128]{3,2,1,0:T(8,128)(2,1)S(1)} %collective-permute-done.1.dn_ref) | copy-start | bytes 688132
  20.4 0.7 copy-start.13
  36.5 17.5 %collective-permute-start.11 = (bf16[38,32,128]{2,1,0:T(8,128)(2,1)S(1)}, bf16[38,32,128]{2,1,0:T(8,128)(2,1)S(1)}, u32[]{:S(2)}, u32[]{:S(2)}) collective-permute-start(bf16[38,32,128]{2,1,0:T(8,128)(2,1)S(1)} %get-tuple-element.42), channel_id=1, source_target_pairs={{28,0},{4,8},{12,16},{60,32},{36,40},{44,48},{92,64},{68,72},{76,8... | collective-permute-start | bytes 933896 | tf_op jit(solution)/shard_map/ppermute | solution.py:292
  37.8 18.1 %collective-permute-start.10 = (bf16[38,32,128]{2,1,0:T(8,128)(2,1)S(1)}, bf16[38,32,128]{2,1,0:T(8,128)(2,1)S(1)}, u32[]{:S(2)}, u32[]{:S(2)}) collective-permute-start(bf16[38,32,128]{2,1,0:T(8,128)(2,1)S(1)} %get-tuple-element.43), channel_id=1, source_target_pairs={{24,0},{0,8},{8,16},{56,32},{32,40},{40,48},{88,64},{64,72},{72,80... | collective-permute-start | bytes 933896 | tf_op jit(solution)/shard_map/ppermute | solution.py:292
  40.6 16.6 %collective-permute-start.9 = (bf16[38,32,128]{2,1,0:T(8,128)(2,1)S(1)}, bf16[38,32,128]{2,1,0:T(8,128)(2,1)S(1)}, u32[]{:S(2)}, u32[]{:S(2)}) collective-permute-start(bf16[38,32,128]{2,1,0:T(8,128)(2,1)S(1)} %get-tuple-element.44), channel_id=1, source_target_pairs={{20,0},{28,8},{4,16},{52,32},{60,40},{36,48},{84,64},{92,72},{68,8... | collective-permute-start | bytes 933896 | tf_op jit(solution)/shard_map/ppermute | solution.py:292
  41.9 15.4 %collective-permute-start.8 = (bf16[38,32,128]{2,1,0:T(8,128)(2,1)S(1)}, bf16[38,32,128]{2,1,0:T(8,128)(2,1)S(1)}, u32[]{:S(2)}, u32[]{:S(2)}) collective-permute-start(bf16[38,32,128]{2,1,0:T(8,128)(2,1)S(1)} %get-tuple-element.45), channel_id=1, source_target_pairs={{16,0},{24,8},{0,16},{48,32},{56,40},{32,48},{80,64},{88,72},{64,8... | collective-permute-start | bytes 933896 | tf_op jit(solution)/shard_map/ppermute | solution.py:292
  44.8 12.5 %collective-permute-start.7 = (bf16[38,32,128]{2,1,0:T(8,128)(2,1)S(1)}, bf16[38,32,128]{2,1,0:T(8,128)(2,1)S(1)}, u32[]{:S(2)}, u32[]{:S(2)}) collective-permute-start(bf16[38,32,128]{2,1,0:T(8,128)(2,1)S(1)} %get-tuple-element.46), channel_id=1, source_target_pairs={{12,0},{20,8},{28,16},{44,32},{52,40},{60,48},{76,64},{84,72},{92,... | collective-permute-start | bytes 933896 | tf_op jit(solution)/shard_map/ppermute | solution.py:292
  54.1 8.8 %copy-start.2 = (bf16[38,32,128]{2,1,0:T(8,128)(2,1)}, bf16[38,32,128]{2,1,0:T(8,128)(2,1)S(1)}, u32[]{:S(2)}) copy-start(bf16[38,32,128]{2,1,0:T(8,128)(2,1)S(1)} %collective-permute-done.11.refs_7_) | copy-start | bytes 933892
  54.1 8.8 %collective-permute-start.6 = (bf16[38,32,128]{2,1,0:T(8,128)(2,1)S(1)}, bf16[38,32,128]{2,1,0:T(8,128)(2,1)S(1)}, u32[]{:S(2)}, u32[]{:S(2)}) collective-permute-start(bf16[38,32,128]{2,1,0:T(8,128)(2,1)S(1)} %get-tuple-element.47), channel_id=1, source_target_pairs={{8,0},{16,8},{24,16},{40,32},{48,40},{56,48},{72,64},{80,72},{88,8... | collective-permute-start | bytes 933896 | tf_op jit(solution)/shard_map/ppermute | solution.py:292
  56.0 6.9 %copy-start.3 = (bf16[38,32,128]{2,1,0:T(8,128)(2,1)}, bf16[38,32,128]{2,1,0:T(8,128)(2,1)S(1)}, u32[]{:S(2)}) copy-start(bf16[38,32,128]{2,1,0:T(8,128)(2,1)S(1)} %collective-permute-done.10.refs_6_) | copy-start | bytes 933892
  56.0 6.9 %collective-permute-start.5 = (bf16[38,32,128]{2,1,0:T(8,128)(2,1)S(1)}, bf16[38,32,128]{2,1,0:T(8,128)(2,1)S(1)}, u32[]{:S(2)}, u32[]{:S(2)}) collective-permute-start(bf16[38,32,128]{2,1,0:T(8,128)(2,1)S(1)} %get-tuple-element.48), channel_id=1, source_target_pairs={{4,0},{12,8},{20,16},{36,32},{44,40},{52,48},{68,64},{76,72},{84,8... | collective-permute-start | bytes 933896 | tf_op jit(solution)/shard_map/ppermute | solution.py:292
  57.3 5.6 %copy-start.4 = (bf16[38,32,128]{2,1,0:T(8,128)(2,1)}, bf16[38,32,128]{2,1,0:T(8,128)(2,1)S(1)}, u32[]{:S(2)}) copy-start(bf16[38,32,128]{2,1,0:T(8,128)(2,1)S(1)} %collective-permute-done.9.refs_5_) | copy-start | bytes 933892
  57.3 5.6 %copy-start.5 = (bf16[38,32,128]{2,1,0:T(8,128)(2,1)}, bf16[38,32,128]{2,1,0:T(8,128)(2,1)S(1)}, u32[]{:S(2)}) copy-start(bf16[38,32,128]{2,1,0:T(8,128)(2,1)S(1)} %collective-permute-done.8.refs_4_) | copy-start | bytes 933892
  57.3 5.6 %copy-start.6 = (bf16[38,32,128]{2,1,0:T(8,128)(2,1)}, bf16[38,32,128]{2,1,0:T(8,128)(2,1)S(1)}, u32[]{:S(2)}) copy-start(bf16[38,32,128]{2,1,0:T(8,128)(2,1)S(1)} %collective-permute-done.7.refs_3_) | copy-start | bytes 933892
  62.9 0.7 copy-start.7
  62.9 0.8 copy-start.8
  67.9 21.1 %collective-permute-start.12 = (bf16[176,32,128]{2,1,0:T(8,128)(2,1)}, bf16[176,32,128]{2,1,0:T(8,128)(2,1)S(1)}, u32[]{:S(2)}, u32[]{:S(2)}) collective-permute-start(bf16[176,32,128]{2,1,0:T(8,128)(2,1)} %get-tuple-element.20), channel_id=1, source_target_pairs={{0,1},{1,2},{2,3},{8,9},{9,10},{10,11},{16,17},{17,18},{18,19},{32... | collective-permute-start | bytes 4325384 | tf_op jit(solution)/shard_map/ppermute | solution.py:304
  69.2 21.4 %collective-permute-start.13 = (bf16[176,32,128]{2,1,0:T(8,128)(2,1)}, bf16[176,32,128]{2,1,0:T(8,128)(2,1)}, u32[]{:S(2)}, u32[]{:S(2)}) collective-permute-start(bf16[176,32,128]{2,1,0:T(8,128)(2,1)} %get-tuple-element.21), channel_id=1, source_target_pairs={{1,0},{2,1},{3,2},{9,8},{10,9},{11,10},{17,16},{18,17},{19,18},{33... | collective-permute-start | bytes 4325384 | tf_op jit(solution)/shard_map/ppermute | solution.py:304
  89.0 3.1 %copy-start.1 = (bf16[176,32,128]{2,1,0:T(8,128)(2,1)}, bf16[176,32,128]{2,1,0:T(8,128)(2,1)S(1)}, u32[]{:S(2)}) copy-start(bf16[176,32,128]{2,1,0:T(8,128)(2,1)S(1)} %collective-permute-done.12.up_ref) | copy-start | bytes 4325380
  105.2 14.6 %collective-permute-start.14 = (f32[16,32,128]{2,1,0:T(8,128)}, f32[16,32,128]{2,1,0:T(8,128)S(1)}, u32[]{:S(2)}, u32[]{:S(2)}) collective-permute-start(f32[16,32,128]{2,1,0:T(8,128)} %get-tuple-element.24), channel_id=1, source_target_pairs={{0,32},{1,33},{2,34},{3,35},{8,40},{9,41},{10,42},{11,43},{16,48},... | collective-permute-start | bytes 786440 | tf_op jit(solution)/shard_map/ppermute | solution.py:304
  108.6 6.0 %collective-permute-start.16 = (bf16[16,32,128]{2,1,0:T(8,128)(2,1)}, bf16[16,32,128]{2,1,0:T(8,128)(2,1)S(1)}, u32[]{:S(2)}, u32[]{:S(2)}) collective-permute-start(bf16[16,32,128]{2,1,0:T(8,128)(2,1)} %get-tuple-element.25), channel_id=1, source_target_pairs={{1,32},{2,33},{3,34},{9,40},{10,41},{11,42},{17,48},{18,49},{19,50... | collective-permute-start | bytes 393224 | tf_op jit(solution)/shard_map/ppermute | solution.py:304
  111.8 8.0 %collective-permute-start.15 = (bf16[16,32,128]{2,1,0:T(8,128)(2,1)}, bf16[16,32,128]{2,1,0:T(8,128)(2,1)S(1)}, u32[]{:S(2)}, u32[]{:S(2)}) collective-permute-start(bf16[16,32,128]{2,1,0:T(8,128)(2,1)} %get-tuple-element.25), channel_id=1, source_target_pairs={{0,33},{1,34},{2,35},{8,41},{9,42},{10,43},{16,49},{17,50},{18,51}... | collective-permute-start | bytes 393224 | tf_op jit(solution)/shard_map/ppermute | solution.py:304
  114.6 5.2 %copy-start.16 = (bf16[16,32,128]{2,1,0:T(8,128)(2,1)}, bf16[16,32,128]{2,1,0:T(8,128)(2,1)S(1)}, u32[]{:S(2)}) copy-start(bf16[16,32,128]{2,1,0:T(8,128)(2,1)S(1)} %collective-permute-done.16.below_ref) | copy-start | bytes 393220
  119.8 0.7 copy-start.18
  120.4 0.7 copy-start.10
  134.4 11.9 %collective-permute-start.17 = (f32[16,32,128]{2,1,0:T(8,128)}, f32[16,32,128]{2,1,0:T(8,128)S(1)}, u32[]{:S(2)}, u32[]{:S(2)}) collective-permute-start(f32[16,32,128]{2,1,0:T(8,128)} %get-tuple-element.26), channel_id=1, source_target_pairs={{0,32},{1,33},{2,34},{3,35},{8,40},{9,41},{10,42},{11,43},{16,48},... | collective-permute-start | bytes 786440 | tf_op jit(solution)/shard_map/ppermute | solution.py:304
  136.4 5.6 %collective-permute-start.19 = (bf16[16,32,128]{2,1,0:T(8,128)(2,1)}, bf16[16,32,128]{2,1,0:T(8,128)(2,1)S(1)}, u32[]{:S(2)}, u32[]{:S(2)}) collective-permute-start(bf16[16,32,128]{2,1,0:T(8,128)(2,1)} %get-tuple-element.27), channel_id=1, source_target_pairs={{1,32},{2,33},{3,34},{9,40},{10,41},{11,42},{17,48},{18,49},{19,50... | collective-permute-start | bytes 393224 | tf_op jit(solution)/shard_map/ppermute | solution.py:304
  137.7 8.6 %collective-permute-start.18 = (bf16[16,32,128]{2,1,0:T(8,128)(2,1)}, bf16[16,32,128]{2,1,0:T(8,128)(2,1)S(1)}, u32[]{:S(2)}, u32[]{:S(2)}) collective-permute-start(bf16[16,32,128]{2,1,0:T(8,128)(2,1)} %get-tuple-element.27), channel_id=1, source_target_pairs={{0,33},{1,34},{2,35},{8,41},{9,42},{10,43},{16,49},{17,50},{18,51}... | collective-permute-start | bytes 393224 | tf_op jit(solution)/shard_map/ppermute | solution.py:304
  141.9 4.3 %copy-start.17 = (bf16[16,32,128]{2,1,0:T(8,128)(2,1)}, bf16[16,32,128]{2,1,0:T(8,128)(2,1)S(1)}, u32[]{:S(2)}) copy-start(bf16[16,32,128]{2,1,0:T(8,128)(2,1)S(1)} %collective-permute-done.19.below_ref) | copy-start | bytes 393220
  146.9 0.7 copy-start.11
  160.7 11.8 %collective-permute-start.20 = (f32[16,32,128]{2,1,0:T(8,128)}, f32[16,32,128]{2,1,0:T(8,128)S(1)}, u32[]{:S(2)}, u32[]{:S(2)}) collective-permute-start(f32[16,32,128]{2,1,0:T(8,128)} %get-tuple-element.28), channel_id=1, source_target_pairs={{0,32},{1,33},{2,34},{3,35},{8,40},{9,41},{10,42},{11,43},{16,48},... | collective-permute-start | bytes 786440 | tf_op jit(solution)/shard_map/ppermute | solution.py:304
  162.6 5.6 %collective-permute-start.22 = (bf16[16,32,128]{2,1,0:T(8,128)(2,1)}, bf16[16,32,128]{2,1,0:T(8,128)(2,1)S(1)}, u32[]{:S(2)}, u32[]{:S(2)}) collective-permute-start(bf16[16,32,128]{2,1,0:T(8,128)(2,1)} %get-tuple-element.29), channel_id=1, source_target_pairs={{1,32},{2,33},{3,34},{9,40},{10,41},{11,42},{17,48},{18,49},{19,50... | collective-permute-start | bytes 393224 | tf_op jit(solution)/shard_map/ppermute | solution.py:304
  163.9 8.6 %collective-permute-start.21 = (bf16[16,32,128]{2,1,0:T(8,128)(2,1)}, bf16[16,32,128]{2,1,0:T(8,128)(2,1)S(1)}, u32[]{:S(2)}, u32[]{:S(2)}) collective-permute-start(bf16[16,32,128]{2,1,0:T(8,128)(2,1)} %get-tuple-element.29), channel_id=1, source_target_pairs={{0,33},{1,34},{2,35},{8,41},{9,42},{10,43},{16,49},{17,50},{18,51}... | collective-permute-start | bytes 393224 | tf_op jit(solution)/shard_map/ppermute | solution.py:304
  168.2 4.3 %copy-start.14 = (bf16[16,32,128]{2,1,0:T(8,128)(2,1)}, bf16[16,32,128]{2,1,0:T(8,128)(2,1)S(1)}, u32[]{:S(2)}) copy-start(bf16[16,32,128]{2,1,0:T(8,128)(2,1)S(1)} %collective-permute-done.22.below_ref) | copy-start | bytes 393220
  173.2 0.7 copy-start.9
  190.0 8.7 %collective-permute-start.23 = (bf16[2,16,32,128]{3,2,1,0:T(8,128)(2,1)}, bf16[2,16,32,128]{3,2,1,0:T(8,128)(2,1)}, u32[]{:S(2)}, u32[]{:S(2)}) collective-permute-start(bf16[2,16,32,128]{3,2,1,0:T(8,128)(2,1)} %get-tuple-element.40), channel_id=1, source_target_pairs={{0,4},{8,12},{16,20},{32,36},{40,44},{48,52},{64,68},{72,76},{80,8... | collective-permute-start | bytes 786440 | tf_op jit(solution)/shard_map/ppermute | solution.py:320
  192.0 9.0 %collective-permute-start.24 = (bf16[2,16,32,128]{3,2,1,0:T(8,128)(2,1)}, bf16[2,16,32,128]{3,2,1,0:T(8,128)(2,1)}, u32[]{:S(2)}, u32[]{:S(2)}) collective-permute-start(bf16[2,16,32,128]{3,2,1,0:T(8,128)(2,1)} %get-tuple-element.39), channel_id=1, source_target_pairs={{0,8},{8,16},{16,24},{32,40},{40,48},{48,56},{64,72},{72,80},{80,8... | collective-permute-start | bytes 786440 | tf_op jit(solution)/shard_map/ppermute | solution.py:320
  194.1 17.0 %collective-permute-start.29 = (bf16[2,16,32,128]{3,2,1,0:T(8,128)(2,1)S(1)}, bf16[2,16,32,128]{3,2,1,0:T(8,128)(2,1)S(1)}, u32[]{:S(2)}, u32[]{:S(2)}) collective-permute-start(bf16[2,16,32,128]{3,2,1,0:T(8,128)(2,1)S(1)} %get-tuple-element.34), channel_id=1, source_target_pairs={{0,28},{8,4},{16,12},{32,60},{40,36},{48,44},{64,92},{72,68},{80,7... | collective-permute-start | bytes 786440 | tf_op jit(solution)/shard_map/ppermute | solution.py:320
  195.4 15.6 %collective-permute-start.28 = (bf16[2,16,32,128]{3,2,1,0:T(8,128)(2,1)}, bf16[2,16,32,128]{3,2,1,0:T(8,128)(2,1)S(1)}, u32[]{:S(2)}, u32[]{:S(2)}) collective-permute-start(bf16[2,16,32,128]{3,2,1,0:T(8,128)(2,1)} %get-tuple-element.35), channel_id=1, source_target_pairs={{0,24},{8,0},{16,8},{32,56},{40,32},{48,40},{64,88},{72,64},{80,72... | collective-permute-start | bytes 786440 | tf_op jit(solution)/shard_map/ppermute | solution.py:320
  197.3 13.7 %collective-permute-start.27 = (bf16[2,16,32,128]{3,2,1,0:T(8,128)(2,1)}, bf16[2,16,32,128]{3,2,1,0:T(8,128)(2,1)S(1)}, u32[]{:S(2)}, u32[]{:S(2)}) collective-permute-start(bf16[2,16,32,128]{3,2,1,0:T(8,128)(2,1)} %get-tuple-element.36), channel_id=1, source_target_pairs={{0,20},{8,28},{16,4},{32,52},{40,60},{48,36},{64,84},{72,92},{80,6... | collective-permute-start | bytes 786440 | tf_op jit(solution)/shard_map/ppermute | solution.py:320
  198.7 7.0 %collective-permute-start.25 = (bf16[2,16,32,128]{3,2,1,0:T(8,128)(2,1)}, bf16[2,16,32,128]{3,2,1,0:T(8,128)(2,1)S(1)}, u32[]{:S(2)}, u32[]{:S(2)}) collective-permute-start(bf16[2,16,32,128]{3,2,1,0:T(8,128)(2,1)} %get-tuple-element.38), channel_id=1, source_target_pairs={{0,12},{8,20},{16,28},{32,44},{40,52},{48,60},{64,76},{72,84},{80,... | collective-permute-start | bytes 786440 | tf_op jit(solution)/shard_map/ppermute | solution.py:320
  201.0 10.0 %collective-permute-start.26 = (bf16[2,16,32,128]{3,2,1,0:T(8,128)(2,1)}, bf16[2,16,32,128]{3,2,1,0:T(8,128)(2,1)S(1)}, u32[]{:S(2)}, u32[]{:S(2)}) collective-permute-start(bf16[2,16,32,128]{3,2,1,0:T(8,128)(2,1)} %get-tuple-element.37), channel_id=1, source_target_pairs={{0,16},{8,24},{16,0},{32,48},{40,56},{48,32},{64,80},{72,88},{80,6... | collective-permute-start | bytes 786440 | tf_op jit(solution)/shard_map/ppermute | solution.py:320
  (2 other events, 1.3 us)
